TPU v7x, 32 devices: a whole 2x2x4 slice. The times are simulated.
32 devices in a mesh: ctx: 8 (over z, core), ch: 4 (over y, x).
Axes of the slice: x: 2, y: 2, z: 4, core: 2. Of those that a mesh axis runs over, the one named last changes fastest.
Arguments:
- token_ids: int32 [1536], P('ctx'), may hold values from 0 to 511
- query_order: int32 [16], replicated, may hold values from 0 to 15, each once
- embed_table: bfloat16 [512, 8192], P(None, 'ch'), may hold values from -36 to 36
- hyena_gain: float32 [8192], P('ch'), may hold values from 0.5 to 1.5
- short_filter: float32 [3, 3, 8192], P(None, None, 'ch'), may hold values from -3 to 3
- decay_rate: float32 [16, 8192], P(None, 'ch'), may hold values from 6.510417e-05 to 0.03125
- residue: float32 [16, 8192], P(None, 'ch'), may hold values from -0.45 to 0.45
- skip_gain: float32 [8192], P('ch'), may hold values from -3 to 3
- attn_gain: float32 [8192], P('ch'), may hold values from 0.5 to 1.5
- w_qkv: bfloat16 [8192, 1536], P('ctx', 'ch'), may hold values from -0.243067956 to 0.243067956
Outputs:
- mixed: bfloat16 [1536, 8192], P('ctx', 'ch')
- attended: bfloat16 [1536, 512], P('ctx', 'ch')
Inputs may be any that keep to these rules, and one draw needn't show every extreme that they name: `query_order`: each of the 16 half-blocks of 96 positions is named exactly once.
All inputs are finite; a program needn't handle non-finite values.
Results may differ from a plain program's by a relative error of at most 0.0085.
Values may be sent and summed in bfloat16 or wider, within the bound.
A program may use at most 192 MiB of HBM per device.

v0:
```python
import math

import jax
import jax.numpy as jnp
from jax import lax
from jax.sharding import PartitionSpec as P

D = 8192
HEAD_DIM = 128
HEAD_DEV = 1
SHORT = 3


def passed_along(block, axis, distance):
    devices = range(lax.axis_size(axis))
    route = [(i - distance, i) for i in devices if i - distance in devices]
    return lax.ppermute(block, axis, route)


def entering(array, axis, combine, identity):
    length, place = (lax.axis_size(axis), lax.axis_index(axis))
    everything = jax.tree.map(lambda part: lax.all_gather(part, axis), array)
    start = jax.tree.map(
        lambda part, zero: jnp.broadcast_to(jnp.asarray(zero, part.dtype), part.shape),
        array,
        identity,
    )

    def lap(k, before):
        reached = k < place
        new = combine(before, jax.tree.map(lambda part: part[k], everything))
        return jax.tree.map(lambda a, b: jnp.where(reached, a, b), new, before)

    return lax.fori_loop(0, length, lap, start)


def rotary(vectors, positions):
    half_dim = vectors.shape[-1] // 2
    frequency = 10000.0 ** (-(jnp.arange(half_dim, dtype=jnp.float32) / half_dim))
    angle = positions.astype(jnp.float32)[:, None] * frequency[None, :]
    cosine = jnp.cos(angle)[:, None, :]
    sine = jnp.sin(angle)[:, None, :]
    first = vectors[..., :half_dim]
    second = vectors[..., half_dim:]
    return jnp.concatenate(
        [first * cosine - second * sine, second * cosine + first * sine], axis=-1
    )


def modal_local(gated, decay_rate, residue, sub_length):
    highest = lax.Precision.HIGHEST
    length = gated.shape[0]
    chan_here = gated.shape[1]
    sub_blocks = length // sub_length
    lag_values = jnp.arange(sub_length, dtype=jnp.float32)
    lag_decay = jnp.exp(-decay_rate[None] * lag_values[:, None, None])
    filter_taps = jnp.einsum("mnc,nc->mc", lag_decay, residue, precision=highest)
    offsets = (
        jnp.arange(sub_length, dtype=jnp.int32)[:, None]
        - jnp.arange(sub_length, dtype=jnp.int32)[None, :]
    )
    selector = (
        offsets[:, :, None] == jnp.arange(sub_length, dtype=jnp.int32)[None, None, :]
    ).astype(jnp.float32)
    toeplitz = jnp.einsum("tsm,mc->tsc", selector, filter_taps, precision=highest)
    pieces = gated.reshape(sub_blocks, sub_length, chan_here)
    inside = jnp.einsum("tsc,qsc->qtc", toeplitz, pieces, precision=highest)
    end_decay = jnp.exp(-decay_rate[None] * (sub_length - 1 - lag_values)[:, None, None])
    sub_ends = jnp.einsum("qsc,snc->qnc", pieces, end_decay, precision=highest)
    sub_index = jnp.arange(sub_blocks, dtype=jnp.int32)
    distance_sub = sub_index[:, None] - 1 - sub_index[None, :]
    spans = (sub_length * jnp.maximum(distance_sub, 0)).astype(jnp.float32)
    carry_weight = jnp.where(
        (distance_sub >= 0)[:, :, None, None],
        jnp.exp(-decay_rate[None, None] * spans[:, :, None, None]),
        0.0,
    )
    local_start = jnp.einsum("qrnc,rnc->qnc", carry_weight, sub_ends, precision=highest)
    tail_span = (sub_length * (sub_blocks - 1 - sub_index)).astype(jnp.float32)
    tail_weight = jnp.exp(-decay_rate[None] * tail_span[:, None, None])
    block_state = jnp.sum(tail_weight * sub_ends, axis=0)
    return (inside, local_start, block_state)


def modal_finish(inside, local_start, incoming, decay_rate, residue, sub_length):
    highest = lax.Precision.HIGHEST
    sub_blocks = inside.shape[0]
    chan_here = inside.shape[2]
    lag_values = jnp.arange(sub_length, dtype=jnp.float32)
    start_span = (sub_length * jnp.arange(sub_blocks, dtype=jnp.int32)).astype(jnp.float32)
    start_decay = jnp.exp(-decay_rate[None] * start_span[:, None, None])
    starts = local_start + start_decay * incoming[None]
    entry_weight = residue[None] * jnp.exp(-decay_rate[None] * (lag_values + 1.0)[:, None, None])
    across = jnp.einsum("qnc,tnc->qtc", starts, entry_weight, precision=highest)
    return (inside + across).reshape(sub_blocks * sub_length, chan_here)


def link_states(earlier, later):
    return (earlier[0] * later[0], earlier[1] * later[0] + later[1])


def make_fold(queries_here, query_positions, scale):
    last_query = jnp.max(query_positions)

    def fold(carry, piece, start):
        key_rows, value_rows = piece
        rows_total = key_rows.shape[0]
        step_rows = 512
        step_count = rows_total // step_rows
        key_steps = key_rows.reshape(step_count, step_rows, HEAD_DEV, HEAD_DIM)
        value_steps = value_rows.reshape(step_count, step_rows, HEAD_DEV, HEAD_DIM)
        first_keys = step_rows * jnp.arange(step_count, dtype=jnp.int32)

        def absorb(state, inputs):
            key_block, value_block, first_key = inputs

            def attend(current):
                out_acc, top_acc, total_acc = current
                key_positions = first_key + jnp.arange(step_rows, dtype=jnp.int32)
                scores = (
                    jnp.einsum(
                        "qhd,khd->hqk", queries_here, key_block, preferred_element_type=jnp.float32
                    )
                    * scale
                )
                allowed = (key_positions[None, :] <= query_positions[:, None])[None]
                masked = jnp.where(allowed, scores, -1e30)
                new_top = jnp.maximum(top_acc, jnp.max(masked, axis=-1))
                weights = jnp.where(allowed, jnp.exp(masked - new_top[..., None]), 0.0)
                rescale = jnp.exp(top_acc - new_top)
                new_total = total_acc * rescale + jnp.sum(weights, axis=-1)
                update = jnp.einsum(
                    "hqk,khd->hqd",
                    weights.astype(jnp.bfloat16),
                    value_block,
                    preferred_element_type=jnp.float32,
                )
                return (out_acc * rescale[..., None] + update, new_top, new_total)

            def unchanged(current):
                return current

            return (lax.cond(first_key <= last_query, attend, unchanged, state), None)

        carry, _ = lax.scan(absorb, carry, (key_steps, value_steps, first_keys))
        return carry

    return fold


def attend_rows(queries_here, query_positions, key_flat, values):
    rows_here = queries_here.shape[0]
    scale = 1.0 / math.sqrt(HEAD_DIM)
    fold = make_fold(queries_here, query_positions, scale)
    initial = (
        jnp.zeros((HEAD_DEV, rows_here, HEAD_DIM), jnp.float32),
        jnp.full((HEAD_DEV, rows_here), -1e30, jnp.float32),
        jnp.zeros((HEAD_DEV, rows_here), jnp.float32),
    )
    out_acc, top_acc, total_acc = fold(
        initial,
        (
            lax.all_gather(key_flat, "ctx", axis=0, tiled=True),
            lax.all_gather(values, "ctx", axis=0, tiled=True),
        ),
        jnp.int32(0),
    )
    context = out_acc / total_acc[..., None]
    return (
        jnp.transpose(context, (1, 0, 2))
        .reshape(rows_here, HEAD_DEV * HEAD_DIM)
        .astype(jnp.bfloat16)
    )


def shards(
    token_ids,
    query_order,
    embed_table,
    hyena_gain,
    short_filter,
    decay_rate,
    residue,
    skip_gain,
    attn_gain,
    w_qkv,
):
    length = token_ids.shape[0]
    vocab_here = embed_table.shape[0]
    nctx = lax.axis_size("ctx")
    rank_here = lax.axis_index("ctx")
    width = HEAD_DEV * HEAD_DIM
    half_rows = length // 2
    sub_length = 32
    onehot = (token_ids[:, None] == jnp.arange(vocab_here, dtype=jnp.int32)[None, :]).astype(
        jnp.bfloat16
    )
    embedded = jnp.dot(onehot, embed_table, preferred_element_type=jnp.float32).astype(jnp.bfloat16)
    embedded_wide = embedded.astype(jnp.float32)
    energy = lax.psum(jnp.sum(embedded_wide * embedded_wide, axis=1), "ch")
    normed = (embedded_wide * lax.rsqrt(energy / D + 1e-06)[:, None] * hyena_gain[None, :]).astype(
        jnp.bfloat16
    )
    earlier_rows = passed_along(normed[length - (SHORT - 1) :], "ctx", 1)
    extended = jnp.concatenate([earlier_rows, normed], axis=0).astype(jnp.float32)
    streams = []
    for stream_index in range(3):
        accum = jnp.zeros(normed.shape, jnp.float32)
        for tap_index in range(SHORT):
            begin = SHORT - 1 - tap_index
            accum = (
                accum
                + short_filter[stream_index, tap_index][None, :] * extended[begin : begin + length]
            )
        streams.append(accum)
    gated = streams[1] * streams[2]
    inside, local_start, block_state = modal_local(gated, decay_rate, residue, sub_length)
    block_decay = jnp.exp(-decay_rate * float(length))
    prefix = entering(
        (block_decay, block_state),
        "ctx",
        link_states,
        (jnp.ones_like(block_decay), jnp.zeros_like(block_state)),
    )
    incoming = prefix[1]
    long_response = modal_finish(inside, local_start, incoming, decay_rate, residue, sub_length)
    mixed = (embedded_wide + streams[0] * (long_response + skip_gain[None, :] * gated)).astype(
        jnp.bfloat16
    )
    mixed_wide = mixed.astype(jnp.float32)
    stream_energy = lax.psum(jnp.sum(mixed_wide * mixed_wide, axis=1), "ch")
    attn_normed = (
        mixed_wide * lax.rsqrt(stream_energy / D + 1e-06)[:, None] * attn_gain[None, :]
    ).astype(jnp.bfloat16)
    normed_full = lax.all_gather(attn_normed, "ch", axis=1, tiled=True)
    projected = jnp.dot(
        normed_full,
        lax.all_gather(w_qkv, "ctx", axis=0, tiled=True),
        preferred_element_type=jnp.float32,
    )
    positions = rank_here * length + jnp.arange(length, dtype=jnp.int32)
    queries = rotary(projected[:, :width].reshape(length, HEAD_DEV, HEAD_DIM), positions).astype(
        jnp.bfloat16
    )
    keys = rotary(
        projected[:, width : 2 * width].reshape(length, HEAD_DEV, HEAD_DIM), positions
    ).astype(jnp.bfloat16)
    values = projected[:, 2 * width :].astype(jnp.bfloat16)
    query_flat = queries.reshape(length, width)
    key_flat = keys.reshape(length, width)
    order_pairs = query_order.reshape(nctx, 2)
    my_blocks = lax.dynamic_index_in_dim(order_pairs, rank_here, 0, False)
    every_query = lax.all_gather(query_flat, "ctx", axis=0, tiled=True)
    first_half = lax.dynamic_slice_in_dim(every_query, my_blocks[0] * half_rows, half_rows, 0)
    second_half = lax.dynamic_slice_in_dim(every_query, my_blocks[1] * half_rows, half_rows, 0)
    my_queries = jnp.concatenate([first_half, second_half], axis=0)
    query_positions = (
        my_blocks[:, None] * half_rows + jnp.arange(half_rows, dtype=jnp.int32)[None, :]
    ).reshape(2 * half_rows)
    attended = attend_rows(
        my_queries.reshape(2 * half_rows, HEAD_DEV, HEAD_DIM), query_positions, key_flat, values
    )
    return (mixed, attended)


def solution(mesh):
    placed = (
        P("ctx"),
        P(),
        P(None, "ch"),
        P("ch"),
        P(None, None, "ch"),
        P(None, "ch"),
        P(None, "ch"),
        P("ch"),
        P("ch"),
        P("ctx", "ch"),
    )
    return jax.shard_map(
        shards,
        mesh=mesh,
        in_specs=placed,
        out_specs=(P("ctx", "ch"), P("ctx", "ch")),
        check_vma=False,
    )
```

profile of v0, /device:TPU:0, one launch (start us, length us, event | category | flops | bytes accessed | tf_op | source)
XLA Modules:
  0.0 431.5 jit_solution(5567717910822324618)
XLA Ops:
  7.2 1.5 copy-done
  8.8 2.5 multiply_reduce_fusion.2
  11.2 11.5 %psum.14 = f32[192]{0:T(256)S(1)} all-reduce(f32[192]{0:T(256)S(1)} %get-tuple-element.406), channel_id=1, replica_groups=mesh['ctx'=8,'ch'=4] {'ch'}, use_global_device_ids=true, to_apply=%region_1.0 | all-reduce | flops 192 | bytes 1536 | tf_op jit(solution)/shard_map/psum | solution.py:200
  22.8 1.6 multiply_convert_fusion
  26.9 1.3 copy.91
  28.3 1.4 maximum_convert_fusion
  29.7 1.9 add_multiply_fusion
  31.6 6.2 %copy.65 = f32[6,32,2048]{1,0,2:T(8,128)} copy(f32[6,32,2048]{2,1,0:T(8,128)} %bitcast.113) | data formatting | bytes 3145728 | tf_op jit(solution)/shard_map/reshape | solution.py:66
  37.8 41.3 %fusion.28 = (f32[16,2048]{0,1:T(8,128)}, f32[2048,16,6]{1,2,0:T(8,128)}) fusion(f32[6]{0:T(128)S(1)} %multiply_convert_fusion.2, f32[16,2048]{0,1:T(8,128)S(1)} %copy.64, f32[6,32,2048]{1,0,2:T(8,128)} %copy.65, f32[32]{0:T(128)S(1)} %iota_subtract_fusion.2), kind=kOutput, calls=%fused_computation.39 | convolution fusion | flops 77103104 | bytes 2621592 | tf_op jit(solution)/shard_map/qsc,snc->qnc/dot_general | solution.py:69
  79.1 2.2 copy.70
  81.4 12.8 %multiply_reduce_fusion = f32[2048,32]{1,0:T(8,128)S(1)} fusion(f32[2048,16]{1,0:T(8,128)} %copy.91, f32[16,2048]{0,1:T(8,128)} %copy-done.3), kind=kLoop, calls=%fused_computation.28 | loop fusion | flops 3080192 | bytes 524288
  95.5 5.8 %fusion.46 = f32[32,32,2048]{2,1,0:T(8,128)} fusion(f32[2048,32]{1,0:T(8,128)S(1)} %multiply_reduce_fusion, s32[32,32]{1,0:T(8,128)S(1)} %iota_subtract_fusion), kind=kOutput, calls=%fused_computation.65 | convolution fusion | flops 805339136 | bytes 8654848 | tf_op jit(solution)/shard_map/tsm,mc->tsc/dot_general | solution.py:65
  101.3 26.3 %copy.66 = f32[32,32,2048]{1,0,2:T(8,128)} copy(f32[32,32,2048]{2,1,0:T(8,128)} %fusion.46) | data formatting | bytes 16777216 | tf_op jit(solution)/shard_map/tsm,mc->tsc/dot_general | solution.py:65
  127.8 4.8 %copy.92 = f32[16,2048,6]{1,0,2:T(8,128)S(1)} copy(f32[16,2048,6]{0,2,1:T(8,128)} %bitcast.112) | data formatting | bytes 1572864
  132.7 2.0 multiply_reduce_fusion.1
  134.7 5.9 %copy.89 = f32[16,2048,6]{0,2,1:T(8,128)} copy(f32[16,2048,6]{1,0,2:T(8,128)} %multiply_reduce_fusion.1) | data formatting | bytes 1572864 | tf_op jit(solution)/shard_map/qrnc,rnc->qnc/dot_general | solution.py:78
  140.6 8.8 %while.30 = (s32[]{:T(128)}, f32[16,2048]{1,0:T(8,128)S(1)}, s32[]{:T(128)}, f32[8,16,2048]{2,1,0:T(8,128)}, f32[8,16,2048]{2,1,0:T(8,128)}, /*index=5*/s32[]{:T(128)}, s32[]{:T(128)}) while((s32[]{:T(128)}, f32[16,2048]{1,0:T(8,128)S(1)}, s32[]{:T(128)}, f32[8,16,2048]{2,1,0:T(8,128)}, f32[8,16,2048]{2,1,0:T(8,128)}, ...), condition=%wide.region_4.5_spmd.clone, body=%wide.region_3.4_spmd.clone.sunk | while | flops 131076 | bytes 524389 | solution.py:34
  150.7 24.2 %fusion.24 = f32[2048,32,6]{1,2,0:T(8,128)S(1)} fusion(f32[16,2048,6]{0,2,1:T(8,128)} %copy.89, f32[32]{0:T(128)S(1)} %iota_add_fusion.2, f32[16,2048]{0,1:T(8,128)} %copy.67, f32[16,2048]{0,1:T(8,128)S(1)} %copy-done.4, f32[16,2048]{0,1:T(8,128)} %copy.71, f32[6]{0:T(128)S(1)} %multiply_convert_fusion.3), kind=kOutput, calls=%fused_computation.32 | convolution fusion | flops 78184448 | bytes 2752664 | tf_op jit(solution)/shard_map/qnc,tnc->qtc/dot_general | solution.py:94
  174.9 57.5 %bitcast_add_fusion.1 = f32[6,32,2048]{1,0,2:T(8,128)} fusion(f32[2048,32,6]{1,2,0:T(8,128)S(1)} %fusion.24, f32[6,32,2048]{1,0,2:T(8,128)} %copy.65, f32[32,32,2048]{1,0,2:T(8,128)} %copy.66), kind=kOutput, calls=%fused_computation.36 | convolution fusion | flops 151388160 | bytes 13107200 | tf_op jit(solution)/shard_map/tsc,qsc->qtc/dot_general | solution.py:67
  232.4 5.9 %copy.72 = f32[6,32,2048]{2,1,0:T(8,128)} copy(f32[6,32,2048]{1,0,2:T(8,128)} %bitcast_add_fusion.1) | data formatting | bytes 3145728 | tf_op jit(solution)/shard_map/add | solution.py:95
  238.3 3.1 fusion.45
  241.7 8.0 %psum.15 = f32[192]{0:T(256)S(1)} all-reduce(f32[192]{0:T(256)S(1)} %fusion.41), channel_id=1, replica_groups=mesh['ctx'=8,'ch'=4] {'ch'}, use_global_device_ids=true, to_apply=%region_6.7 | all-reduce | flops 192 | bytes 1536 | tf_op jit(solution)/shard_map/psum | solution.py:231
  254.3 42.1 %all-gather.7.cloned.1.call-done = bf16[192,8192]{1,0:T(8,128)(2,1)} async-done(((bf16[192,2048]{1,0:T(8,128)(2,1)}), bf16[192,8192]{1,0:T(8,128)(2,1)}) %all-gather.7.cloned.1.call-update) | async-done | bytes 3145744 | tf_op jit(solution)/shard_map/all_gather | solution.py:235
  296.4 66.2 %all-gather.9.cloned.1.call-done = bf16[8192,384]{1,0:T(8,128)(2,1)} async-done(((bf16[1024,384]{1,0:T(8,128)(2,1)}), bf16[8192,384]{1,0:T(8,128)(2,1)}) %all-gather.9.cloned.1.call-update) | async-done | bytes 6291472 | tf_op jit(solution)/shard_map/all_gather | solution.py:238
  362.6 5.5 %fusion.75 = f32[192,384]{1,0:T(8,128)S(1)} fusion(bf16[192,8192]{1,0:T(8,128)(2,1)} %all-gather.7.cloned.1.call-done, bf16[8192,384]{1,0:T(8,128)(2,1)} %all-gather.9.cloned.1.call-done), kind=kOutput, calls=%fused_computation.125 | convolution fusion | flops 1207959552 | bytes 9732096 | tf_op jit(solution)/shard_map/dot_general | solution.py:236
  368.8 14.5 %all_gather.34 = bf16[1536,128]{1,0:T(8,128)(2,1)S(1)} all-gather(bf16[192,128]{1,0:T(8,128)(2,1)S(1)} %pad_maximum_fusion.1), channel_id=1, replica_groups=mesh['ctx'=8,'ch'=4] {'ctx'}, dimensions={0}, use_global_device_ids=true | all-gather | bytes 442368 | tf_op jit(solution)/shard_map/all_gather | solution.py:253
  383.4 14.5 %all_gather.33 = bf16[1536,128]{1,0:T(8,128)(2,1)S(1)} all-gather(bf16[192,128]{1,0:T(8,128)(2,1)S(1)} %pad_maximum_fusion), channel_id=1, replica_groups=mesh['ctx'=8,'ch'=4] {'ctx'}, dimensions={0}, use_global_device_ids=true | all-gather | bytes 442368 | tf_op jit(solution)/shard_map/all_gather | solution.py:163
  397.8 14.4 %all_gather.35 = bf16[1536,128]{1,0:T(8,128)(2,1)S(1)} all-gather(bf16[192,128]{1,0:T(8,128)(2,1)S(1)} %slice.141), channel_id=1, replica_groups=mesh['ctx'=8,'ch'=4] {'ctx'}, dimensions={0}, use_global_device_ids=true | all-gather | bytes 442368 | tf_op jit(solution)/shard_map/all_gather | solution.py:164
  412.3 10.8 %while.29 = (s32[]{:T(128)}, f32[1,192,128]{2,1,0:T(8,128)S(1)}, f32[1,192]{1,0:T(1,128)S(1)}, f32[1,192]{1,0:T(1,128)S(1)}, s32[3]{0:T(128)S(1)}, /*index=5*/s3...) while((s32[]{:T(128)}, f32[1,192,128]{2,1,0:T(8,128)S(1)}, ...), condition=%wide.region_13.14_spmd.clone, body=%wide.region_8.13_spmd.clone.sunk | while | flops 51561540 | bytes 1715491 | solution.py:145
  414.2 1.7 conditional.3
  417.8 1.7 conditional.3
  421.4 1.7 conditional.3
  (115 shorter events, 26.6 us)
Async XLA Ops:
  7.2 1.6 copy-start
  7.2 15.6 %copy-start.9 = (f32[2048]{0:T(1024)S(1)}, f32[2048]{0:T(1024)}, u32[]{:S(2)}) copy-start(f32[2048]{0:T(1024)} %param.19) | copy-start | bytes 24580
  7.2 133.4 %all-gather.11.cloned.1.call-start = ((), (), s32[]{:S(2)}) async-start(), calls=%async_computation.2 | async-start | bytes 1179648 | tf_op jit(solution)/shard_map/all_gather | solution.py:22
  11.2 14.5 %copy-start.7 = (f32[16,2048]{1,0:T(8,128)S(1)}, f32[16,2048]{1,0:T(8,128)}, u32[]{:S(2)}) copy-start(f32[16,2048]{1,0:T(8,128)} %param.21) | copy-start | bytes 393220
  11.2 15.3 %copy-start.8 = (f32[3,3,2048]{2,1,0:T(4,128)S(1)}, f32[3,3,2048]{2,1,0:T(4,128)}, u32[]{:S(2)}) copy-start(f32[3,3,2048]{2,1,0:T(4,128)} %param.20) | copy-start | bytes 221188
  22.8 4.2 copy-start.6
  24.4 3.9 copy-start.5
  24.4 3.9 collective-permute-start
  26.4 114.1 %all-gather.13.cloned.1.call-start = ((), (), s32[]{:S(2)}) async-start(), calls=%async_computation.3 | async-start | bytes 1179648 | tf_op jit(solution)/shard_map/all_gather | solution.py:22
  26.9 10.9 %copy-start.3 = (f32[16,2048]{0,1:T(8,128)}, f32[16,2048]{0,1:T(8,128)S(1)}, u32[]{:S(2)}) copy-start(f32[16,2048]{0,1:T(8,128)S(1)} %copy.64) | copy-start | bytes 393220
  81.4 215.1 %all-gather.7.cloned.1.call-start = ((), (), s32[]{:S(2)}) async-start(), calls=%async_computation | async-start | bytes 3932160 | tf_op jit(solution)/shard_map/all_gather | solution.py:235
  140.6 10.1 %copy-start.4 = (f32[16,2048]{0,1:T(8,128)S(1)}, f32[16,2048]{0,1:T(8,128)}, u32[]{:S(2)}) copy-start(f32[16,2048]{0,1:T(8,128)} %copy-done.3) | copy-start | bytes 393220
  232.4 5.9 %copy-start.11 = (f32[2048]{0:T(1024)S(1)}, f32[2048]{0:T(1024)}, u32[]{:S(2)}) copy-start(f32[2048]{0:T(1024)} %param.23) | copy-start | bytes 24580
  238.3 11.4 %copy-start.10 = (f32[2048]{0:T(1024)S(1)}, f32[2048]{0:T(1024)}, u32[]{:S(2)}) copy-start(f32[2048]{0:T(1024)} %param.24) | copy-start | bytes 24580
  241.5 10.0 %copy-start.2 = (bf16[192,2048]{1,0:T(8,128)(2,1)}, bf16[192,2048]{1,0:T(8,128)(2,1)S(1)}, u32[]{:S(2)}) copy-start(bf16[192,2048]{1,0:T(8,128)(2,1)S(1)} %fusion.45) | copy-start | bytes 2359300
  241.7 9.8 %copy-start.12 = (s32[16]{0:T(128)S(1)}, s32[16]{0:T(128)}, u32[]{:S(2)}) copy-start(s32[16]{0:T(128)} %param.17) | copy-start | bytes 196
  250.9 111.7 %all-gather.9.cloned.1.call-start = ((), (), s32[]{:S(2)}) async-start(), calls=%async_computation.1 | async-start | bytes 7077888 | tf_op jit(solution)/shard_map/all_gather | solution.py:238
  423.1 1.6 copy-start.1
Sparse Core Ops, SparseCore 0:
  26.6 22.5 all-gather.10
  81.5 22.7 all-gather.12
  251.0 45.3 all-gather.6
  297.9 64.6 all-gather.8
where the time goes:
time: 436 us; the launch traced here: 432 us
  matrix products  139 us (32%)
  waiting for transfers between devices  109 us (25%)
  blocking collectives  62.9 us (14%)
  local copies, waits for them, and re-layouts  61.1 us (14%)
  other arithmetic  38.8 us (9%)
  between operations  15.6 us (4%)
    all_gather x1, waiting for transfers between devices, shards(): lax.all_gather(w_qkv, 'ctx', axis=0, tiled=True)  66.2 us
    dot_general x1, matrix products, modal_local(): inside = jnp.einsum('tsc,qsc->qtc', toeplitz, pieces, precision=highest)  57.5 us
    all_gather x1, waiting for transfers between devices, shards(): normed_full = lax.all_gather(attn_normed, 'ch', axis=1, tiled=True)  42.1 us
    dot_general x1, matrix products, modal_local(): sub_ends = jnp.einsum('qsc,snc->qnc', pieces, end_decay, precision=highest)  41.3 us
    dot_general x1, local copies, waits for them, and re-layouts, modal_local(): jnp.einsum('tsm,mc->tsc', selector, filter_taps, precision=highest)  26.3 us
    dot_general x1, matrix products, modal_finish(): across = jnp.einsum('qnc,tnc->qtc', starts, entry_weight, precision=highest)  24.2 us
    unnamed x3, other arithmetic  14.8 us
    all_gather x1, blocking collectives, shards(): every_query = lax.all_gather(query_flat, 'ctx', axis=0, tiled=True)  14.5 us
  transfers between devices with their start and end apart: 5, of which 2 were waited for; matrix products, arithmetic and copies ran while one was open for 27% of the time, Pallas kernels for 0%

commit v1 on v0

v1 whole, which is shorter than its diff:
```python
import functools
import math

import jax
import jax.numpy as jnp
from jax import lax
from jax.experimental import pallas as pl
from jax.experimental.pallas import tpu as pltpu
from jax.sharding import PartitionSpec as P

D = 8192
HEAD_DIM = 128
HEAD_DEV = 1
SHORT = 3
ORDER = 16
HALO = 16
SPAN_MOST = 1024


def modal_local(
    ids_ref,
    scale_ref,
    table_ref,
    gain_ref,
    taps_ref,
    decay_ref,
    residue_ref,
    skip_ref,
    query_ref,
    base_ref,
    state_ref,
    normed_ref,
    gated_ref,
    long_ref,
):
    rows = query_ref.shape[0]
    vocab, span = table_ref.shape
    tiles = span // 128
    padded = ids_ref.shape[0]
    onehot = (
        (ids_ref[...] == lax.broadcasted_iota(jnp.int32, (padded, vocab), 1))
        .astype(jnp.float32)
        .astype(jnp.bfloat16)
    )
    embedded = jnp.dot(onehot, table_ref[...], preferred_element_type=jnp.float32)
    base_ref[...] = embedded[HALO:]
    normed_ref[...] = (
        (embedded * scale_ref[...] * gain_ref[...]).astype(jnp.bfloat16).astype(jnp.float32)
    )
    taps = taps_ref[...]

    def stream(j):
        total = taps[3 * j : 3 * j + 1] * normed_ref[HALO:]
        for i in range(1, SHORT):
            k = 3 * j + i
            total = total + taps[k : k + 1] * normed_ref[HALO - i : HALO - i + rows]
        return total

    query = stream(0)
    gated = stream(1) * stream(2)
    query_ref[...] = query
    base_ref[...] += query * (skip_ref[...] * gated)
    for r in range(rows // 8):
        for k in range(tiles):
            gated_ref[(r * tiles + k) * 8 : (r * tiles + k + 1) * 8, :] = gated[
                r * 8 : r * 8 + 8, k * 128 : k * 128 + 128
            ]
    decay = [jnp.exp(-decay_ref[n]) for n in range(ORDER)]

    def step(r, states):
        states = list(states)
        for t in range(8):
            place = pl.ds(r * (8 * tiles) + t, tiles, stride=8)
            entry = gated_ref[place, :]
            terms = []
            for n in range(ORDER):
                states[n] = decay[n] * states[n] + entry
                terms.append(residue_ref[n] * states[n])
            while len(terms) > 1:
                terms = [a + b for a, b in zip(terms[::2], terms[1::2])]
            long_ref[place, :] = terms[0]
        return tuple(states)

    zero = jnp.zeros((tiles, 128), jnp.float32)
    states = lax.fori_loop(0, rows // 8, step, (zero,) * ORDER)
    for n in range(ORDER):
        state_ref[n] = states[n]
    for r in range(rows // 8):
        for k in range(tiles):
            spot = (slice(r * 8, r * 8 + 8), slice(k * 128, k * 128 + 128))
            base_ref[spot] += (
                query_ref[spot] * long_ref[(r * tiles + k) * 8 : (r * tiles + k + 1) * 8, :]
            )


def modal_finish(
    rank_ref,
    states_ref,
    decay_ref,
    residue_ref,
    query_ref,
    base_ref,
    gain_ref,
    mixed_ref,
    scaled_ref,
    energy_ref,
    long_ref,
):
    rows, span = query_ref.shape
    tiles = span // 128
    rank = rank_ref[0]
    block_decay = [jnp.exp(-decay_ref[n] * float(rows)) for n in range(ORDER)]

    def carry(k, states):
        return tuple(states[n] * block_decay[n] + states_ref[k, n] for n in range(ORDER))

    zero = jnp.zeros((tiles, 128), jnp.float32)
    incoming = lax.fori_loop(0, rank, carry, (zero,) * ORDER)
    decay = [jnp.exp(-decay_ref[n]) for n in range(ORDER)]

    def step(r, terms):
        terms = list(terms)
        for t in range(8):
            terms = [decay[n] * terms[n] for n in range(ORDER)]
            sums = terms
            while len(sums) > 1:
                sums = [a + b for a, b in zip(sums[::2], sums[1::2])]
            long_ref[pl.ds(r * (8 * tiles) + t, tiles, stride=8), :] = sums[0]
        return tuple(terms)

    lax.fori_loop(
        0, rows // 8, step, tuple(residue_ref[n] * incoming[n] for n in range(ORDER))
    )
    @pl.when(pl.program_id(0) == 0)
    def _():
        energy_ref[...] = jnp.zeros_like(energy_ref)

    for r in range(rows // 16):
        energy = jnp.zeros((16, 128), jnp.float32)
        for k in range(tiles):
            spot = (slice(r * 16, r * 16 + 16), slice(k * 128, k * 128 + 128))
            first = (2 * r * tiles + k) * 8
            second = ((2 * r + 1) * tiles + k) * 8
            late = jnp.concatenate(
                [long_ref[first : first + 8, :], long_ref[second : second + 8, :]], axis=0
            )
            mixed = (base_ref[spot] + query_ref[spot] * late).astype(jnp.bfloat16)
            mixed_ref[spot] = mixed
            wide = mixed.astype(jnp.float32)
            scaled_ref[spot] = (wide * gain_ref[:, spot[1]]).astype(jnp.bfloat16)
            energy = energy + wide * wide
        energy_ref[r * 16 : r * 16 + 16, :] += energy


def attend(blocks_ref, qkv_ref, out_ref):
    half_rows = out_ref.shape[0] // 2
    keys_total = qkv_ref.shape[0]
    width = HEAD_DIM
    for b in range(2):
        start = pl.multiple_of(blocks_ref[b] * half_rows, 32)
        queries = qkv_ref[pl.ds(start, half_rows), :width]
        keys = qkv_ref[:, width : 2 * width]
        values = qkv_ref[:, 2 * width :]
        scores = lax.dot_general(
            queries, keys, (((1,), (1,)), ((), ())), preferred_element_type=jnp.float32
        ) * (1.0 / math.sqrt(HEAD_DIM))
        at = start + lax.broadcasted_iota(jnp.int32, (half_rows, keys_total), 0)
        allowed = lax.broadcasted_iota(jnp.int32, (half_rows, keys_total), 1) <= at
        masked = jnp.where(allowed, scores, -1e30)
        top = jnp.max(masked, axis=1, keepdims=True)
        weights = jnp.where(allowed, jnp.exp(masked - top), 0.0)
        total = jnp.sum(weights, axis=1, keepdims=True)
        out = jnp.dot(weights.astype(jnp.bfloat16), values, preferred_element_type=jnp.float32)
        out_ref[b * half_rows : (b + 1) * half_rows, :] = (out / total).astype(jnp.bfloat16)


def rotate(vectors, cosine, sine):
    half_dim = HEAD_DIM // 2
    first = vectors[:, :half_dim]
    second = vectors[:, half_dim:]
    return jnp.concatenate(
        [first * cosine - second * sine, second * cosine + first * sine], axis=1
    )


def shards(
    token_ids,
    query_order,
    embed_table,
    hyena_gain,
    short_filter,
    decay_rate,
    residue,
    skip_gain,
    attn_gain,
    w_qkv,
):
    length = token_ids.shape[0]
    vocab = embed_table.shape[0]
    here = embed_table.shape[1]
    span = min(SPAN_MOST, here)
    spans = here // span
    tiles = span // 128
    nctx = lax.axis_size("ctx")
    rank = lax.axis_index("ctx")
    padded = length + HALO
    weights_full = lax.all_gather(w_qkv, "ctx", axis=0, tiled=True)
    earlier_ids = lax.ppermute(
        token_ids[length - HALO :], "ctx", [(i, i + 1) for i in range(nctx - 1)]
    )
    ids = jnp.concatenate([earlier_ids, token_ids])
    table_wide = embed_table.astype(jnp.float32)
    table_energy = lax.psum(jnp.sum(table_wide * table_wide, axis=1), "ch")
    energy = jnp.sum(
        jnp.where(
            ids[:, None] == jnp.arange(vocab, dtype=jnp.int32)[None, :], table_energy[None, :], 0.0
        ),
        axis=1,
    )
    real = (jnp.arange(padded) >= HALO) | (rank > 0)
    scale = jnp.where(real, lax.rsqrt(energy / D + 1e-06), 0.0)
    decay_tiles = decay_rate.reshape(ORDER, spans, tiles, 128).swapaxes(0, 1)
    residue_tiles = residue.reshape(ORDER, spans, tiles, 128).swapaxes(0, 1)
    row = lambda size: pl.BlockSpec((size, span), lambda h: (0, h))
    tile = pl.BlockSpec((None, ORDER, tiles, 128), lambda h: (h, 0, 0, 0))
    lone = lambda size: pl.BlockSpec((size, 1), lambda h: (0, 0))
    query, base, state = pl.pallas_call(
        modal_local,
        grid=(spans,),
        in_specs=[
            lone(padded), lone(padded), row(vocab), row(1), row(9), tile, tile, row(1)
        ],
        out_specs=[row(length), row(length), tile],
        out_shape=[
            jax.ShapeDtypeStruct((length, here), jnp.float32),
            jax.ShapeDtypeStruct((length, here), jnp.float32),
            jax.ShapeDtypeStruct((spans, ORDER, tiles, 128), jnp.float32),
        ],
        scratch_shapes=[
            pltpu.VMEM((padded, span), jnp.float32),
            pltpu.VMEM((length * tiles, 128), jnp.float32),
            pltpu.VMEM((length * tiles, 128), jnp.float32),
        ],
        name="modal_local",
    )(
        ids[:, None],
        scale[:, None],
        embed_table,
        hyena_gain[None],
        short_filter.reshape(9, here),
        decay_tiles,
        residue_tiles,
        skip_gain[None],
    )
    states = lax.all_gather(state, "ctx")
    mixed, scaled, lanes = pl.pallas_call(
        modal_finish,
        grid_spec=pltpu.PrefetchScalarGridSpec(
            num_scalar_prefetch=1,
            grid=(spans,),
            in_specs=[
                pl.BlockSpec((nctx, None, ORDER, tiles, 128), lambda h, s: (0, h, 0, 0, 0)),
                pl.BlockSpec((None, ORDER, tiles, 128), lambda h, s: (h, 0, 0, 0)),
                pl.BlockSpec((None, ORDER, tiles, 128), lambda h, s: (h, 0, 0, 0)),
                pl.BlockSpec((length, span), lambda h, s: (0, h)),
                pl.BlockSpec((length, span), lambda h, s: (0, h)),
                pl.BlockSpec((1, span), lambda h, s: (0, h)),
            ],
            out_specs=[
                pl.BlockSpec((length, span), lambda h, s: (0, h)),
                pl.BlockSpec((length, span), lambda h, s: (0, h)),
                pl.BlockSpec((length, 128), lambda h, s: (0, 0)),
            ],
            scratch_shapes=[pltpu.VMEM((length * tiles, 128), jnp.float32)],
        ),
        out_shape=[
            jax.ShapeDtypeStruct((length, here), jnp.bfloat16),
            jax.ShapeDtypeStruct((length, here), jnp.bfloat16),
            jax.ShapeDtypeStruct((length, 128), jnp.float32),
        ],
        name="modal_finish",
    )(rank[None], states, decay_tiles, residue_tiles, query, base, attn_gain[None])
    stream_energy = lax.psum(jnp.sum(lanes, axis=1), "ch")
    row_scale = lax.rsqrt(stream_energy / D + 1e-06)[:, None]
    scaled_full = lax.all_gather(scaled, "ch", axis=1, tiled=True)
    projected = (
        jnp.dot(scaled_full, weights_full, preferred_element_type=jnp.float32) * row_scale
    )
    half_dim = HEAD_DIM // 2
    positions = rank * length + jnp.arange(length, dtype=jnp.int32)
    frequency = 10000.0 ** (-(jnp.arange(half_dim, dtype=jnp.float32) / half_dim))
    angle = positions.astype(jnp.float32)[:, None] * frequency[None, :]
    cosine, sine = jnp.cos(angle), jnp.sin(angle)
    width = HEAD_DIM
    qkv = jnp.concatenate(
        [
            rotate(projected[:, :width], cosine, sine),
            rotate(projected[:, width : 2 * width], cosine, sine),
            projected[:, 2 * width :],
        ],
        axis=1,
    ).astype(jnp.bfloat16)
    every = lax.all_gather(qkv, "ctx", axis=0, tiled=True)
    blocks = lax.dynamic_slice_in_dim(query_order, rank * 2, 2)
    attended = pl.pallas_call(
        attend,
        in_specs=[
            pl.BlockSpec(memory_space=pltpu.SMEM),
            pl.BlockSpec(memory_space=pltpu.VMEM),
        ],
        out_specs=pl.BlockSpec(memory_space=pltpu.VMEM),
        out_shape=jax.ShapeDtypeStruct((length, width), jnp.bfloat16),
        name="attend",
    )(blocks, every)
    return (mixed, attended)


def solution(mesh):
    placed = (
        P("ctx"),
        P(),
        P(None, "ch"),
        P("ch"),
        P(None, None, "ch"),
        P(None, "ch"),
        P(None, "ch"),
        P("ch"),
        P("ch"),
        P("ctx", "ch"),
    )
    return jax.shard_map(
        shards,
        mesh=mesh,
        in_specs=placed,
        out_specs=(P("ctx", "ch"), P("ctx", "ch")),
        check_vma=False,
    )
```

time: 436 us -> 214 us (0.49)
  matrix products: 139 us -> 5.54 us
  local copies, waits for them, and re-layouts: 61.1 us -> 7.18 us
  blocking collectives: 62.9 us -> 20.7 us
  other arithmetic: 38.8 us -> 4.51 us
  waiting for transfers between devices: 109 us -> 142 us
  Pallas kernels: 0 us -> 17.3 us
    dot_general x12 -> x1, matrix products: 139 us -> 5.54 us  [shards(): jnp.dot(scaled_full, weights_full, preferred_element_type=jnp.float32)]
    all_gather x3 -> x0, blocking collectives: 43.4 us -> none  [the longest x1 14.5 us: shards(): every_query = lax.all_gather(query_flat, 'ctx', axis=0, tiled=True)]
    all_gather x4, waiting for transfers between devices: 108 us -> 141 us  [the longest x1 66.4 us: shards(): weights_full = lax.all_gather(w_qkv, 'ctx', axis=0, tiled=True)]
    dot_general x2 -> x0, local copies, waits for them, and re-layouts: 32.2 us -> none  [the longest x1 26.3 us: modal_local(): jnp.einsum('tsm,mc->tsc', selector, filter_taps, precision=highest)]
    pallas_call x0 -> x3, Pallas kernels: none -> 17.3 us  [the longest x1 9.42 us: shards(): pl.pallas_call(modal_local, grid=(spans,), in_specs=[lone(padded), lone(p...]
    unnamed x3 -> x0, other arithmetic: 14.8 us -> none
    unnamed x29 -> x6, local copies, waits for them, and re-layouts: 9.98 us -> 1.87 us
    select_n x8 -> x1, other arithmetic: 8.65 us -> 0.64 us  [shards(): scale = jnp.where(real, lax.rsqrt(energy / D + 1e-06), 0.0)]
  transfers between devices with their start and end apart: 5 -> 5, of which waited for: 2 -> 4; matrix products, arithmetic and copies ran while one was open for 27% -> 4% of each run, Pallas kernels for 0% -> 0%
where the time goes in v1:
time: 214 us; the launch traced here: 213 us
  waiting for transfers between devices  142 us (66%)
  blocking collectives  20.7 us (10%)
  Pallas kernels  17.3 us (8%)
  between operations  13.9 us (6%)
  local copies, waits for them, and re-layouts  7.18 us (3%)
  matrix products  5.54 us (3%)
  other arithmetic  4.51 us (2%)
  starting transfers between devices  2.54 us (1%)
    all_gather x1, waiting for transfers between devices, shards(): weights_full = lax.all_gather(w_qkv, 'ctx', axis=0, tiled=True)  66.4 us
    all_gather x1, waiting for transfers between devices, shards(): scaled_full = lax.all_gather(scaled, 'ch', axis=1, tiled=True)  31.9 us
    all_gather x1, waiting for transfers between devices, shards(): states = lax.all_gather(state, 'ctx')  21.9 us
    all_gather x1, waiting for transfers between devices, shards(): every = lax.all_gather(qkv, 'ctx', axis=0, tiled=True)  21 us
    psum x1, blocking collectives, shards(): table_energy = lax.psum(jnp.sum(table_wide * table_wide, axis=1), 'ch')  10.7 us
    psum x1, blocking collectives, shards(): stream_energy = lax.psum(jnp.sum(lanes, axis=1), 'ch')  9.94 us
    pallas_call x1, Pallas kernels, shards(): pl.pallas_call(modal_local, grid=(spans,), in_specs=[lone(padded), lone(p...  9.42 us
    dot_general x1, matrix products, shards(): jnp.dot(scaled_full, weights_full, preferred_element_type=jnp.float32)  5.54 us
  transfers between devices with their start and end apart: 5, of which 4 were waited for; matrix products, arithmetic and copies ran while one was open for 4% of the time, Pallas kernels for 0%

profile of v1, /device:TPU:0, one launch (start us, length us, event | category | flops | bytes accessed | tf_op | source)
XLA Modules:
  0.0 213.5 jit_solution(10546566775451686580)
XLA Ops:
  7.2 0.0 all-gather.12.cloned.1.call-start
  7.2 0.8 slice.25
  8.0 2.4 %collective-permute-start = (s32[16]{0:T(128)S(1)}, s32[16]{0:T(128)S(1)}, u32[]{:S(2)}, u32[]{:S(2)}) collective-permute-start(s32[16]{0:T(128)S(1)} %slice.25), channel_id=1, source_target_pairs={{0,4},{4,8},{8,12},{12,16},{16,20},{20,24},{24,28},{1,5},{5,9},{9,... | collective-permute-start | bytes 200 | tf_op jit(solution)/shard_map/ppermute | solution.py:208
  10.4 2.1 multiply_reduce_fusion
  12.5 10.7 %psum.14 = f32[512]{0:T(512)S(1)} all-reduce(f32[512]{0:T(512)S(1)} %multiply_reduce_fusion), channel_id=1, replica_groups=mesh['ctx'=8,'ch'=4] {'ch'}, use_global_device_ids=true, to_apply=%region_1.0 | all-reduce | flops 512 | bytes 4096 | tf_op jit(solution)/shard_map/psum | solution.py:213
  23.2 0.9 copy.24
  24.1 0.9 copy.25
  25.1 1.6 reshape.58.taps_ref
  26.7 0.7 copy_bitcast_fusion
  27.4 0.1 pad_add_fusion
  27.5 0.2 select_reduce_fusion
  27.7 0.1 copy.20
  27.8 0.8 copy.23.ids_ref
  28.6 0.6 fusion.9.scale_ref
  29.2 9.4 %modal_local.1 = (f32[192,2048]{1,0:T(8,128)}, f32[192,2048]{1,0:T(8,128)}, f32[2,16,8,128]{3,2,1,0:T(8,128)}) custom-call(s32[208,1]{1,0:T(8,128)} %copy.23.ids_ref, f32[208,1]{1,0:T(8,128)} %fusion.9.scale_ref, bf16[512,2048]{1,0:T(8,128)(2,1)} %table_ref.1, f32[1,2048]{1,0:T(1,128)} %bitcast.25, f32[9,2048]{1,0:T(8,128)} %reshape.58.taps_ref, ...), custom_call_target="tpu_custom_call" | custom-call | tf_op jit(solution)/shard_map/modal_local/pallas_call | solution.py:227
  38.7 0.0 all-gather.12.cloned.1.call-update
  38.7 0.0 all-gather.6.cloned.1.call-start
  38.7 21.9 %all-gather.12.cloned.1.call-done = f32[16,16,8,128]{3,2,1,0:T(8,128)} async-done(((f32[2,16,8,128]{3,2,1,0:T(8,128)}), f32[16,16,8,128]{3,2,1,0:T(8,128)}) %all-gather.12.cloned.1.call-update) | async-done | bytes 1048592 | tf_op jit(solution)/shard_map/all_gather | solution.py:255
  60.6 4.8 %modal_finish.1 = (bf16[192,2048]{1,0:T(8,128)(2,1)}, bf16[192,2048]{1,0:T(8,128)(2,1)}, f32[192,128]{1,0:T(8,128)}) custom-call(s32[1]{0:T(128)} %bitcast.rank_ref, f32[8,2,16,8,128]{4,3,2,1,0:T(8,128)} %bitcast.19, f32[2,16,8,128]{3,2,1,0:T(8,128)} %get-tuple-element.19.decay_ref, f32[2,16,8,128]{3,2,1,0:T(8,128)} %get-tuple-element.18.residue_ref, ...), custom_call_target="tpu_custom_call" | custom-call | tf_op jit(solution)/shard_map/modal_finish/pallas_call | solution.py:256
  65.5 0.0 all-gather.8.cloned.1.call-start
  65.5 0.7 all-gather.8.cloned.1.call-update
  66.2 0.0 all-gather.10.cloned.1.call-start
  66.3 1.0 reduce_sum.29
  67.3 9.9 %psum.15 = f32[192]{0:T(256)S(1)} all-reduce(f32[192]{0:T(256)S(1)} %reduce_sum.29), channel_id=1, replica_groups=mesh['ctx'=8,'ch'=4] {'ch'}, use_global_device_ids=true, to_apply=%region_4.5 | all-reduce | flops 192 | bytes 1536 | tf_op jit(solution)/shard_map/psum | solution.py:283
  77.3 31.9 %all-gather.6.cloned.1.call-done = bf16[192,8192]{1,0:T(8,128)(2,1)} async-done(((bf16[192,2048]{1,0:T(8,128)(2,1)}), bf16[192,8192]{1,0:T(8,128)(2,1)}) %all-gather.6.cloned.1.call-update) | async-done | bytes 3145744 | tf_op jit(solution)/shard_map/all_gather | solution.py:285
  109.1 66.4 %all-gather.8.cloned.1.call-done = bf16[8192,384]{1,0:T(8,128)(2,1)} async-done(((bf16[1024,384]{1,0:T(8,128)(2,1)}), bf16[8192,384]{1,0:T(8,128)(2,1)}) %all-gather.8.cloned.1.call-update) | async-done | bytes 6291472 | tf_op jit(solution)/shard_map/all_gather | solution.py:207
  175.5 5.5 %convolution_multiply_fusion = f32[192,384]{1,0:T(8,128)S(1)} fusion(bf16[192,8192]{1,0:T(8,128)(2,1)} %all-gather.6.cloned.1.call-done, bf16[8192,384]{1,0:T(8,128)(2,1)} %all-gather.8.cloned.1.call-done, f32[192]{0:T(256)S(1)} %add_rsqrt_fusion), kind=kOutput, calls=%fused_computation.1 | convolution fusion | flops 1208033280 | bytes 9732864 | tf_op jit(solution)/shard_map/dot_general | solution.py:287
  181.1 0.5 fusion.17
  181.6 0.8 concatenate.8
  182.4 0.6 dynamic_slice.3.blocks_ref
  182.9 21.0 %all-gather.10.cloned.1.call-done.qkv_ref = bf16[1536,384]{1,0:T(8,128)(2,1)} async-done(((bf16[192,384]{1,0:T(8,128)(2,1)}), bf16[1536,384]{1,0:T(8,128)(2,1)}) %all-gather.10.cloned.1.call-update) | async-done | bytes 1179664 | tf_op jit(solution)/shard_map/all_gather | solution.py:303
  203.9 3.0 %attend.1 = bf16[192,128]{1,0:T(8,128)(2,1)} custom-call(s32[2]{0:T(128)} %dynamic_slice.3.blocks_ref, bf16[1536,384]{1,0:T(8,128)(2,1)} %all-gather.10.cloned.1.call-done.qkv_ref), custom_call_target="tpu_custom_call" | custom-call | tf_op jit(solution)/shard_map/attend/pallas_call | solution.py:305
  (12 shorter events, 0.1 us)
Async XLA Ops:
  7.2 20.2 %copy-start = (s32[192]{0:T(256)S(1)}, s32[192]{0:T(256)}, u32[]{:S(2)}) copy-start(s32[192]{0:T(256)} %param.10) | copy-start | bytes 2308
  7.2 53.5 %all-gather.12.cloned.1.call-start = ((), (), s32[]{:S(2)}) async-start(), calls=%async_computation.3 | async-start | bytes 1179648 | tf_op jit(solution)/shard_map/all_gather | solution.py:255
  8.0 19.4 %collective-permute-start = (s32[16]{0:T(128)S(1)}, s32[16]{0:T(128)S(1)}, u32[]{:S(2)}, u32[]{:S(2)}) collective-permute-start(s32[16]{0:T(128)S(1)} %slice.25), channel_id=1, source_target_pairs={{0,4},{4,8},{8,12},{12,16},{16,20},{20,24},{24,28},{1,5},{5,9},{9,... | collective-permute-start | bytes 200 | tf_op jit(solution)/shard_map/ppermute | solution.py:208
  38.7 70.5 %all-gather.6.cloned.1.call-start = ((), (), s32[]{:S(2)}) async-start(), calls=%async_computation | async-start | bytes 3932160 | tf_op jit(solution)/shard_map/all_gather | solution.py:285
  65.5 110.0 %all-gather.8.cloned.1.call-start = ((), (), s32[]{:S(2)}) async-start(), calls=%async_computation.1 | async-start | bytes 7077888 | tf_op jit(solution)/shard_map/all_gather | solution.py:207
  66.2 137.7 %all-gather.10.cloned.1.call-start = ((), (), s32[]{:S(2)}) async-start(), calls=%async_computation.2 | async-start | bytes 1327104 | tf_op jit(solution)/shard_map/all_gather | solution.py:303
  77.3 105.1 %copy-start.1 = (s32[16]{0:T(128)S(1)}, s32[16]{0:T(128)}, u32[]{:S(2)}) copy-start(s32[16]{0:T(128)} %param.11) | copy-start | bytes 196
Sparse Core Ops, SparseCore 0:
  38.8 21.7 all-gather.11
  65.6 43.4 all-gather.5
  110.8 64.6 all-gather.7
  182.5 21.4 all-gather.9

commit v2 on v1

--- a/solution.py
+++ b/solution.py
@@ -10,7 +10,6 @@
 
 D = 8192
 HEAD_DIM = 128
-HEAD_DEV = 1
 SHORT = 3
 ORDER = 16
 HALO = 16
@@ -131,6 +130,7 @@
     lax.fori_loop(
         0, rows // 8, step, tuple(residue_ref[n] * incoming[n] for n in range(ORDER))
     )
+
     @pl.when(pl.program_id(0) == 0)
     def _():
         energy_ref[...] = jnp.zeros_like(energy_ref)
@@ -150,6 +150,135 @@
             scaled_ref[spot] = (wide * gain_ref[:, spot[1]]).astype(jnp.bfloat16)
             energy = energy + wide * wide
         energy_ref[r * 16 : r * 16 + 16, :] += energy
+
+
+def direct_kernel(axis, columns, count, *refs):
+    ins, outs = refs[:count], refs[count : 2 * count]
+    send, recv, own = refs[2 * count :]
+    size, me = lax.axis_size(axis), lax.axis_index(axis)
+    barrier = pltpu.get_barrier_semaphore()
+    for d in range(1, size):
+        peer = lax.rem(me + d, size)
+        pl.semaphore_signal(
+            barrier, inc=1, device_id={axis: peer}, device_id_type=pl.DeviceIdType.MESH
+        )
+    pl.semaphore_wait(barrier, size - 1)
+    copies = []
+    for a in range(count):
+        if columns[a]:
+            width = ins[a].shape[1]
+            spot = outs[a].at[:, pl.ds(pl.multiple_of(me * width, 128), width)]
+        else:
+            spot = outs[a].at[me]
+        for d in range(1, size):
+            copies.append(
+                pltpu.make_async_remote_copy(
+                    src_ref=ins[a],
+                    dst_ref=spot,
+                    send_sem=send.at[a, d - 1],
+                    recv_sem=recv.at[a, d - 1],
+                    device_id={axis: lax.rem(me + d, size)},
+                    device_id_type=pl.DeviceIdType.MESH,
+                )
+            )
+        copies.append(pltpu.make_async_copy(ins[a], spot, own.at[a]))
+    for copy in copies:
+        copy.start()
+    for copy in copies:
+        copy.wait()
+
+
+def paired_kernel(axis, in_ref, out_ref, send, recv, hand_send, hand_recv, own):
+    size, me = lax.axis_size(axis), lax.axis_index(axis)
+    chips = size // 2
+    chip, core = lax.div(me, 2), lax.rem(me, 2)
+    sibling = me + 1 - 2 * core
+    peers = [sibling] + [lax.rem(chip + d, chips) * 2 + core for d in range(1, chips)]
+    barrier = pltpu.get_barrier_semaphore()
+    for peer in peers:
+        pl.semaphore_signal(
+            barrier, inc=1, device_id={axis: peer}, device_id_type=pl.DeviceIdType.MESH
+        )
+    pl.semaphore_wait(barrier, chips)
+    copies = [
+        pltpu.make_async_remote_copy(
+            src_ref=in_ref,
+            dst_ref=out_ref.at[me],
+            send_sem=send.at[d],
+            recv_sem=recv.at[d],
+            device_id={axis: peers[d]},
+            device_id_type=pl.DeviceIdType.MESH,
+        )
+        for d in range(chips)
+    ]
+    for copy in copies[1:]:
+        copy.start()
+    copies[0].start()
+    mine = pltpu.make_async_copy(in_ref, out_ref.at[me], own)
+    mine.start()
+    hands = []
+    for d in range(1, chips):
+        copies[d].wait_recv()
+        source = lax.rem(chip + chips - d, chips) * 2 + core
+        hand = pltpu.make_async_remote_copy(
+            src_ref=out_ref.at[source],
+            dst_ref=out_ref.at[source],
+            send_sem=hand_send.at[d],
+            recv_sem=hand_recv.at[d],
+            device_id={axis: sibling},
+            device_id_type=pl.DeviceIdType.MESH,
+        )
+        hand.start()
+        hands.append(hand)
+    mine.wait()
+    copies[0].wait_recv()
+    for copy in copies:
+        copy.wait_send()
+    for hand in hands:
+        hand.wait()
+
+
+def gather_direct(axis, arrays, columns, collective_id):
+    size, count = lax.axis_size(axis), len(arrays)
+    vmem = pl.BlockSpec(memory_space=pltpu.VMEM)
+    dma = pltpu.SemaphoreType.DMA
+    return pl.pallas_call(
+        functools.partial(direct_kernel, axis, columns, count),
+        in_specs=[vmem] * count,
+        out_specs=[vmem] * count,
+        out_shape=[
+            jax.ShapeDtypeStruct(
+                (a.shape[0], size * a.shape[1]) if wide else (size,) + a.shape, a.dtype
+            )
+            for a, wide in zip(arrays, columns)
+        ],
+        scratch_shapes=[dma((count, size - 1)), dma((count, size - 1)), dma((count,))],
+        compiler_params=pltpu.CompilerParams(
+            collective_id=collective_id, has_side_effects=True
+        ),
+    )(*arrays)
+
+
+def gather_paired(axis, array, collective_id):
+    size = lax.axis_size(axis)
+    vmem = pl.BlockSpec(memory_space=pltpu.VMEM)
+    dma = pltpu.SemaphoreType.DMA
+    chips = size // 2
+    return pl.pallas_call(
+        functools.partial(paired_kernel, axis),
+        in_specs=[vmem],
+        out_specs=vmem,
+        out_shape=jax.ShapeDtypeStruct((size,) + array.shape, array.dtype),
+        scratch_shapes=[dma((chips,)), dma((chips,)), dma((chips,)), dma((chips,)), dma(())],
+        compiler_params=pltpu.CompilerParams(
+            collective_id=collective_id, has_side_effects=True
+        ),
+    )(array)
+
+
+def packed(vector):
+    wide = -(-vector.shape[0] // 1024) * 1024
+    return jnp.pad(vector, (0, wide - vector.shape[0])).reshape(wide // 128, 128)
 
 
 def attend(blocks_ref, qkv_ref, out_ref):
@@ -210,7 +339,10 @@
     )
     ids = jnp.concatenate([earlier_ids, token_ids])
     table_wide = embed_table.astype(jnp.float32)
-    table_energy = lax.psum(jnp.sum(table_wide * table_wide, axis=1), "ch")
+    (table_parts,) = gather_direct(
+        "ch", [packed(jnp.sum(table_wide * table_wide, axis=1))], (False,), 1
+    )
+    table_energy = jnp.sum(table_parts, axis=0).reshape(-1)[:vocab]
     energy = jnp.sum(
         jnp.where(
             ids[:, None] == jnp.arange(vocab, dtype=jnp.int32)[None, :], table_energy[None, :], 0.0
@@ -224,7 +356,7 @@
     row = lambda size: pl.BlockSpec((size, span), lambda h: (0, h))
     tile = pl.BlockSpec((None, ORDER, tiles, 128), lambda h: (h, 0, 0, 0))
     lone = lambda size: pl.BlockSpec((size, 1), lambda h: (0, 0))
-    query, base, state = pl.pallas_call(
+    local = pl.pallas_call(
         modal_local,
         grid=(spans,),
         in_specs=[
@@ -242,7 +374,8 @@
             pltpu.VMEM((length * tiles, 128), jnp.float32),
         ],
         name="modal_local",
-    )(
+    )
+    local_args = (
         ids[:, None],
         scale[:, None],
         embed_table,
@@ -252,7 +385,10 @@
         residue_tiles,
         skip_gain[None],
     )
-    states = lax.all_gather(state, "ctx")
+    query, base, state = local(*local_args)
+    states = gather_paired(
+        "ctx", state.reshape(spans * ORDER * tiles, 128), 2
+    ).reshape(nctx, spans, ORDER, tiles, 128)
     mixed, scaled, lanes = pl.pallas_call(
         modal_finish,
         grid_spec=pltpu.PrefetchScalarGridSpec(
@@ -280,9 +416,11 @@
         ],
         name="modal_finish",
     )(rank[None], states, decay_tiles, residue_tiles, query, base, attn_gain[None])
-    stream_energy = lax.psum(jnp.sum(lanes, axis=1), "ch")
+    scaled_full, energy_parts = gather_direct(
+        "ch", [scaled, packed(jnp.sum(lanes, axis=1))], (True, False), 3
+    )
+    stream_energy = jnp.sum(energy_parts, axis=0).reshape(-1)[:length]
     row_scale = lax.rsqrt(stream_energy / D + 1e-06)[:, None]
-    scaled_full = lax.all_gather(scaled, "ch", axis=1, tiled=True)
     projected = (
         jnp.dot(scaled_full, weights_full, preferred_element_type=jnp.float32) * row_scale
     )
@@ -300,7 +438,7 @@
         ],
         axis=1,
     ).astype(jnp.bfloat16)
-    every = lax.all_gather(qkv, "ctx", axis=0, tiled=True)
+    every = gather_paired("ctx", qkv, 4).reshape(nctx * length, 3 * width)
     blocks = lax.dynamic_slice_in_dim(query_order, rank * 2, 2)
     attended = pl.pallas_call(
         attend,

time: 214 us -> 153 us (0.71)
  waiting for transfers between devices: 142 us -> 0.69 us
  Pallas kernels: 17.3 us -> 116 us
  blocking collectives: 20.7 us -> 0 us
    pallas_call x1 -> x5, Pallas kernels: 9.42 us -> 108 us  [the longest x2 51.2 us: gather_paired(): pl.pallas_call(functools.partial(paired_kernel, axis), in_specs=[vmem], o...]
    all_gather x3 -> x0, waiting for transfers between devices: 74.8 us -> none  [the longest x1 31.9 us: shards(): scaled_full = lax.all_gather(scaled, 'ch', axis=1, tiled=True)]
    all_gather x1, waiting for transfers between devices: 66.4 us -> 0.01 us  [shards(): weights_full = lax.all_gather(w_qkv, 'ctx', axis=0, tiled=True)]
    psum x2 -> x0, blocking collectives: 20.7 us -> none  [the longest x1 10.7 us: shards(): table_energy = lax.psum(jnp.sum(table_wide * table_wide, axis=1), 'ch')]
    reduce_sum x2 -> x4, other arithmetic: 3.08 us -> 4.53 us  [the longest x1 2.08 us: shards(): jnp.sum(table_wide * table_wide, axis=1)]
  transfers between devices with their start and end apart: 5 -> 2, of which waited for: 4 -> 0; matrix products, arithmetic and copies ran while one was open for 4% -> 7% of each run, Pallas kernels for 0% -> 57%
where the time goes in v2:
time: 153 us; the launch traced here: 151 us
  Pallas kernels  116 us (76%)
  between operations  14.2 us (9%)
  local copies, waits for them, and re-layouts  6.59 us (4%)
  other arithmetic  5.96 us (4%)
  matrix products  5.54 us (4%)
  starting transfers between devices  2.42 us (2%)
    pallas_call x2, Pallas kernels, gather_paired(): pl.pallas_call(functools.partial(paired_kernel, axis), in_specs=[vmem], o...  51.2 us
    pallas_call x2, Pallas kernels, gather_direct(): pl.pallas_call(functools.partial(direct_kernel, axis, columns, count), in...  47.6 us
    pallas_call x1, Pallas kernels, shards(): query, base, state = local(*local_args)  9.43 us
    dot_general x1, matrix products, shards(): jnp.dot(scaled_full, weights_full, preferred_element_type=jnp.float32)  5.54 us
    pallas_call x1, Pallas kernels, shards(): pl.pallas_call(modal_finish, grid_spec=pltpu.PrefetchScalarGridSpec(num_s...  4.86 us
  transfers between devices with their start and end apart: 2, of which 0 were waited for; matrix products, arithmetic and copies ran while one was open for 7% of the time, Pallas kernels for 57%

profile of v2, /device:TPU:0, one launch (start us, length us, event | category | flops | bytes accessed | tf_op | source)
XLA Modules:
  0.0 151.5 jit_solution(14261717830785192570)
XLA Ops:
  7.2 0.0 all-gather.2.cloned.1.call-start
  7.2 0.7 all-gather.2.cloned.1.call-update
  7.9 0.8 slice.32
  8.7 2.4 %collective-permute-start = (s32[16]{0:T(128)S(1)}, s32[16]{0:T(128)S(1)}, u32[]{:S(2)}, u32[]{:S(2)}) collective-permute-start(s32[16]{0:T(128)S(1)} %slice.32), channel_id=1, source_target_pairs={{0,4},{4,8},{8,12},{12,16},{16,20},{20,24},{24,28},{1,5},{5,9},{9,... | collective-permute-start | bytes 200 | tf_op jit(solution)/shard_map/ppermute | solution.py:337
  11.1 2.1 %multiply_reduce_fusion = f32[512]{0:T(512)S(1)} fusion(bf16[512,2048]{1,0:T(8,128)(2,1)} %table_ref.1), kind=kLoop, calls=%fused_computation | loop fusion | flops 3145216 | bytes 2099200 | tf_op jit(solution)/shard_map/reduce_sum | solution.py:343
  13.2 0.6 pad_bitcast_fusion.1.refs_0_
  13.8 6.8 %shard_map.113 = f32[4,8,128]{2,1,0:T(8,128)} custom-call(f32[8,128]{1,0:T(8,128)} %pad_bitcast_fusion.1.refs_0_), custom_call_target="tpu_custom_call" | custom-call | tf_op jit(solution)/shard_map/pallas_call | solution.py:245
  20.6 0.9 copy.20
  21.5 0.0 copy-done
  21.6 0.7 reshape.80.taps_ref
  22.3 0.7 reduce_sum.46
  23.0 0.7 copy_bitcast_fusion
  23.7 0.6 dynamic_slice.3.blocks_ref
  24.3 0.0 collective-permute-done
  24.3 0.1 pad_add_fusion
  24.4 0.2 select_reduce_fusion
  24.6 0.1 copy.16
  24.7 0.8 copy.19.ids_ref
  25.5 0.6 fusion.9.scale_ref
  26.1 9.4 %modal_local.1 = (f32[192,2048]{1,0:T(8,128)}, f32[192,2048]{1,0:T(8,128)}, f32[2,16,8,128]{3,2,1,0:T(8,128)}) custom-call(s32[208,1]{1,0:T(8,128)} %copy.19.ids_ref, f32[208,1]{1,0:T(8,128)} %fusion.9.scale_ref, bf16[512,2048]{1,0:T(8,128)(2,1)} %table_ref.1, f32[1,2048]{1,0:T(1,128)} %bitcast.36, f32[9,2048]{1,0:T(8,128)} %reshape.80.taps_ref, ...), custom_call_target="tpu_custom_call" | custom-call | tf_op jit(solution)/shard_map/modal_local/pallas_call | solution.py:388
  35.6 24.1 %shard_map.114 = f32[8,256,128]{2,1,0:T(8,128)} custom-call(f32[256,128]{1,0:T(8,128)} %bitcast.32), custom_call_target="tpu_custom_call" | custom-call | tf_op jit(solution)/shard_map/pallas_call | solution.py:267
  59.7 4.9 %modal_finish.1 = (bf16[192,2048]{1,0:T(8,128)(2,1)}, bf16[192,2048]{1,0:T(8,128)(2,1)}, f32[192,128]{1,0:T(8,128)}) custom-call(s32[1]{0:T(128)} %bitcast.rank_ref, f32[8,2,16,8,128]{4,3,2,1,0:T(8,128)} %bitcast.29, f32[2,16,8,128]{3,2,1,0:T(8,128)} %get-tuple-element.23.decay_ref, f32[2,16,8,128]{3,2,1,0:T(8,128)} %get-tuple-element.22.residue_ref, ...), custom_call_target="tpu_custom_call" | custom-call | tf_op jit(solution)/shard_map/modal_finish/pallas_call | solution.py:392
  64.5 1.0 reduce_sum.48
  65.5 0.6 pad_bitcast_fusion.refs_1_
  66.1 40.8 %shard_map.115 = (bf16[192,8192]{1,0:T(8,128)(2,1)}, f32[4,8,128]{2,1,0:T(8,128)}) custom-call(bf16[192,2048]{1,0:T(8,128)(2,1)} %get-tuple-element.14.refs_0_, f32[8,128]{1,0:T(8,128)} %pad_bitcast_fusion.refs_1_), custom_call_target="tpu_custom_call" | custom-call | tf_op jit(solution)/shard_map/pallas_call | solution.py:245
  106.9 0.7 reduce_sum.49
  107.7 0.0 all-gather.2.cloned.1.call-done
  107.7 5.5 %convolution_multiply_fusion = f32[192,384]{1,0:T(8,128)S(1)} fusion(bf16[192,8192]{1,0:T(8,128)(2,1)} %get-tuple-element.16, bf16[8192,384]{1,0:T(8,128)(2,1)} %all-gather.2.cloned.1.call-done, f32[192]{0:T(256)S(1)} %add_rsqrt_fusion), kind=kOutput, calls=%fused_computation.1 | convolution fusion | flops 1208033280 | bytes 9732864 | tf_op jit(solution)/shard_map/dot_general | solution.py:425
  113.2 0.5 fusion.17
  113.7 0.8 concatenate.8.in_ref
  114.5 27.1 %shard_map.116 = bf16[8,192,384]{2,1,0:T(8,128)(2,1)} custom-call(bf16[192,384]{1,0:T(8,128)(2,1)} %concatenate.8.in_ref), custom_call_target="tpu_custom_call" | custom-call | tf_op jit(solution)/shard_map/pallas_call | solution.py:267
  141.6 3.0 %attend.1 = bf16[192,128]{1,0:T(8,128)(2,1)} custom-call(s32[2]{0:T(128)} %dynamic_slice.3.blocks_ref, bf16[1536,384]{1,0:T(8,128)(2,1)} %bitcast.28), custom_call_target="tpu_custom_call" | custom-call | tf_op jit(solution)/shard_map/attend/pallas_call | solution.py:443
  (14 shorter events, 0.1 us)
Async XLA Ops:
  7.2 17.1 %copy-start.2 = (s32[192]{0:T(256)S(1)}, s32[192]{0:T(256)}, u32[]{:S(2)}) copy-start(s32[192]{0:T(256)} %param.10) | copy-start | bytes 2308
  7.2 14.3 %copy-start = (f32[16,2048]{1,0:T(8,128)S(1)}, f32[16,2048]{1,0:T(8,128)}, u32[]{:S(2)}) copy-start(f32[16,2048]{1,0:T(8,128)} %param.16) | copy-start | bytes 393220
  7.2 14.4 %copy-start.1 = (f32[3,3,2048]{2,1,0:T(4,128)S(1)}, f32[3,3,2048]{2,1,0:T(4,128)}, u32[]{:S(2)}) copy-start(f32[3,3,2048]{2,1,0:T(4,128)} %param.14) | copy-start | bytes 221188
  7.2 16.5 %copy-start.3 = (s32[16]{0:T(128)S(1)}, s32[16]{0:T(128)}, u32[]{:S(2)}) copy-start(s32[16]{0:T(128)} %param.11) | copy-start | bytes 196
  7.2 100.5 %all-gather.2.cloned.1.call-start = ((), (), s32[]{:S(2)}) async-start(), calls=%async_computation | async-start | bytes 7077888 | tf_op jit(solution)/shard_map/all_gather | solution.py:336
  8.7 15.6 %collective-permute-start = (s32[16]{0:T(128)S(1)}, s32[16]{0:T(128)S(1)}, u32[]{:S(2)}, u32[]{:S(2)}) collective-permute-start(s32[16]{0:T(128)S(1)} %slice.32), channel_id=1, source_target_pairs={{0,4},{4,8},{8,12},{12,16},{16,20},{20,24},{24,28},{1,5},{5,9},{9,... | collective-permute-start | bytes 200 | tf_op jit(solution)/shard_map/ppermute | solution.py:337
Sparse Core Ops, SparseCore 0:
  9.7 78.3 all-gather.1

commit v3 on v2

--- a/solution.py
+++ b/solution.py
@@ -83,7 +83,7 @@
     zero = jnp.zeros((tiles, 128), jnp.float32)
     states = lax.fori_loop(0, rows // 8, step, (zero,) * ORDER)
     for n in range(ORDER):
-        state_ref[n] = states[n]
+        state_ref[n] = states[n].astype(state_ref.dtype)
     for r in range(rows // 8):
         for k in range(tiles):
             spot = (slice(r * 8, r * 8 + 8), slice(k * 128, k * 128 + 128))
@@ -111,7 +111,7 @@
     block_decay = [jnp.exp(-decay_ref[n] * float(rows)) for n in range(ORDER)]
 
     def carry(k, states):
-        return tuple(states[n] * block_decay[n] + states_ref[k, n] for n in range(ORDER))
+        return tuple(states[n] * block_decay[n] + states_ref[k, n].astype(jnp.float32) for n in range(ORDER))
 
     zero = jnp.zeros((tiles, 128), jnp.float32)
     incoming = lax.fori_loop(0, rank, carry, (zero,) * ORDER)
@@ -188,6 +188,72 @@
         copy.wait()
 
 
+def square_kernel(
+    axis, in_ref, small_ref, out_ref, small_out_ref, send, recv, small_send, small_recv, own
+):
+    me = lax.axis_index(axis)
+    y, x = lax.div(me, 2), lax.rem(me, 2)
+    beside, above = y * 2 + 1 - x, (1 - y) * 2 + x
+    peers = [beside, above, (1 - y) * 2 + 1 - x]
+    barrier = pltpu.get_barrier_semaphore()
+    for peer in peers:
+        pl.semaphore_signal(
+            barrier, inc=1, device_id={axis: peer}, device_id_type=pl.DeviceIdType.MESH
+        )
+    pl.semaphore_wait(barrier, 3)
+    rows, width = in_ref.shape
+    half = rows // 2
+
+    def spot(owner, part):
+        return out_ref.at[
+            part * half : (part + 1) * half, pl.ds(pl.multiple_of(owner * width, 128), width)
+        ]
+
+    def remote(source, target, slot, peer):
+        return pltpu.make_async_remote_copy(
+            src_ref=source,
+            dst_ref=target,
+            send_sem=send.at[slot],
+            recv_sem=recv.at[slot],
+            device_id={axis: peer},
+            device_id_type=pl.DeviceIdType.MESH,
+        )
+
+    parts = [in_ref.at[:half], in_ref.at[half:]]
+    first = remote(parts[0], spot(me, 0), 0, beside)
+    second = remote(parts[1], spot(me, 1), 1, above)
+    third = remote(parts[1], spot(me, 1), 2, beside)
+    fourth = remote(parts[0], spot(me, 0), 3, above)
+    small = [
+        pltpu.make_async_remote_copy(
+            src_ref=small_ref,
+            dst_ref=small_out_ref.at[me],
+            send_sem=small_send.at[d],
+            recv_sem=small_recv.at[d],
+            device_id={axis: peers[d]},
+            device_id_type=pl.DeviceIdType.MESH,
+        )
+        for d in range(3)
+    ]
+    mine = [
+        pltpu.make_async_copy(parts[0], spot(me, 0), own.at[0]),
+        pltpu.make_async_copy(parts[1], spot(me, 1), own.at[1]),
+        pltpu.make_async_copy(small_ref, small_out_ref.at[me], own.at[2]),
+    ]
+    for copy in [first, second] + small + [third, fourth] + mine:
+        copy.start()
+    first.wait_recv()
+    onward = remote(spot(beside, 0), spot(beside, 0), 4, above)
+    onward.start()
+    second.wait_recv()
+    across = remote(spot(above, 1), spot(above, 1), 5, beside)
+    across.start()
+    first.wait_send()
+    second.wait_send()
+    for copy in [third, fourth] + small + mine + [onward, across]:
+        copy.wait()
+
+
 def paired_kernel(axis, in_ref, out_ref, send, recv, hand_send, hand_recv, own):
     size, me = lax.axis_size(axis), lax.axis_index(axis)
     chips = size // 2
@@ -257,6 +323,27 @@
             collective_id=collective_id, has_side_effects=True
         ),
     )(*arrays)
+
+
+def gather_square(axis, array, small, collective_id):
+    size = lax.axis_size(axis)
+    if size != 4:
+        return gather_direct(axis, [array, small], (True, False), collective_id)
+    vmem = pl.BlockSpec(memory_space=pltpu.VMEM)
+    dma = pltpu.SemaphoreType.DMA
+    return pl.pallas_call(
+        functools.partial(square_kernel, axis),
+        in_specs=[vmem, vmem],
+        out_specs=[vmem, vmem],
+        out_shape=[
+            jax.ShapeDtypeStruct((array.shape[0], size * array.shape[1]), array.dtype),
+            jax.ShapeDtypeStruct((size,) + small.shape, small.dtype),
+        ],
+        scratch_shapes=[dma((6,)), dma((6,)), dma((3,)), dma((3,)), dma((3,))],
+        compiler_params=pltpu.CompilerParams(
+            collective_id=collective_id, has_side_effects=True
+        ),
+    )(array, small)
 
 
 def gather_paired(axis, array, collective_id):
@@ -366,7 +453,7 @@
         out_shape=[
             jax.ShapeDtypeStruct((length, here), jnp.float32),
             jax.ShapeDtypeStruct((length, here), jnp.float32),
-            jax.ShapeDtypeStruct((spans, ORDER, tiles, 128), jnp.float32),
+            jax.ShapeDtypeStruct((spans, ORDER, tiles, 128), jnp.bfloat16),
         ],
         scratch_shapes=[
             pltpu.VMEM((padded, span), jnp.float32),
@@ -416,9 +503,7 @@
         ],
         name="modal_finish",
     )(rank[None], states, decay_tiles, residue_tiles, query, base, attn_gain[None])
-    scaled_full, energy_parts = gather_direct(
-        "ch", [scaled, packed(jnp.sum(lanes, axis=1))], (True, False), 3
-    )
+    scaled_full, energy_parts = gather_square("ch", scaled, packed(jnp.sum(lanes, axis=1)), 3)
     stream_energy = jnp.sum(energy_parts, axis=0).reshape(-1)[:length]
     row_scale = lax.rsqrt(stream_energy / D + 1e-06)[:, None]
     projected = (

time: 153 us -> 131 us (0.86)
  Pallas kernels: 116 us -> 94.5 us
    pallas_call x2 -> x1, Pallas kernels: 47.6 us -> 6.8 us  [gather_direct(): pl.pallas_call(functools.partial(direct_kernel, axis, columns, count), in...]
    pallas_call x0 -> x1, Pallas kernels: none -> 32.4 us  [gather_square(): pl.pallas_call(functools.partial(square_kernel, axis), in_specs=[vmem, vm...]
    pallas_call x2, Pallas kernels: 51.2 us -> 38.1 us  [gather_paired(): pl.pallas_call(functools.partial(paired_kernel, axis), in_specs=[vmem], o...]
  transfers between devices with their start and end apart: 2 -> 2, of which waited for: 0 -> 0; matrix products, arithmetic and copies ran while one was open for 7% -> 9% of each run, Pallas kernels for 57% -> 53%
where the time goes in v3:
time: 131 us; the launch traced here: 130 us
  Pallas kernels  94.5 us (72%)
  between operations  14.2 us (11%)
  local copies, waits for them, and re-layouts  6.64 us (5%)
  other arithmetic  5.96 us (5%)
  matrix products  5.54 us (4%)
  starting transfers between devices  2.42 us (2%)
    pallas_call x2, Pallas kernels, gather_paired(): pl.pallas_call(functools.partial(paired_kernel, axis), in_specs=[vmem], o...  38.1 us
    pallas_call x1, Pallas kernels, gather_square(): pl.pallas_call(functools.partial(square_kernel, axis), in_specs=[vmem, vm...  32.4 us
    pallas_call x1, Pallas kernels, shards(): query, base, state = local(*local_args)  9.42 us
    pallas_call x1, Pallas kernels, gather_direct(): pl.pallas_call(functools.partial(direct_kernel, axis, columns, count), in...  6.8 us
    dot_general x1, matrix products, shards(): jnp.dot(scaled_full, weights_full, preferred_element_type=jnp.float32)  5.54 us
    pallas_call x1, Pallas kernels, shards(): pl.pallas_call(modal_finish, grid_spec=pltpu.PrefetchScalarGridSpec(num_s...  4.8 us
    pallas_call x1, Pallas kernels, shards(): pl.pallas_call(attend, in_specs=[pl.BlockSpec(memory_space=pltpu.SMEM), p...  3.02 us
  transfers between devices with their start and end apart: 2, of which 0 were waited for; matrix products, arithmetic and copies ran while one was open for 9% of the time, Pallas kernels for 53%

profile of v3, /device:TPU:0, one launch (start us, length us, event | category | flops | bytes accessed | tf_op | source)
XLA Modules:
  0.0 130.0 jit_solution(8337142713550781257)
XLA Ops:
  7.2 0.0 all-gather.2.cloned.1.call-start
  7.2 0.7 all-gather.2.cloned.1.call-update
  7.9 0.8 slice.32
  8.7 2.4 %collective-permute-start = (s32[16]{0:T(128)S(1)}, s32[16]{0:T(128)S(1)}, u32[]{:S(2)}, u32[]{:S(2)}) collective-permute-start(s32[16]{0:T(128)S(1)} %slice.32), channel_id=1, source_target_pairs={{0,4},{4,8},{8,12},{12,16},{16,20},{20,24},{24,28},{1,5},{5,9},{9,... | collective-permute-start | bytes 200 | tf_op jit(solution)/shard_map/ppermute | solution.py:424
  11.1 2.1 %multiply_reduce_fusion = f32[512]{0:T(512)S(1)} fusion(bf16[512,2048]{1,0:T(8,128)(2,1)} %table_ref.1), kind=kLoop, calls=%fused_computation | loop fusion | flops 3145216 | bytes 2099200 | tf_op jit(solution)/shard_map/reduce_sum | solution.py:430
  13.2 0.6 pad_bitcast_fusion.1.refs_0_
  13.8 6.8 %shard_map.113 = f32[4,8,128]{2,1,0:T(8,128)} custom-call(f32[8,128]{1,0:T(8,128)} %pad_bitcast_fusion.1.refs_0_), custom_call_target="tpu_custom_call" | custom-call | tf_op jit(solution)/shard_map/pallas_call | solution.py:311
  20.6 0.9 copy.20
  21.5 0.0 copy-done
  21.6 0.7 reshape.80.taps_ref
  22.3 0.7 reduce_sum.46
  23.0 0.7 copy_bitcast_fusion
  23.8 0.6 dynamic_slice.3.blocks_ref
  24.3 0.0 collective-permute-done
  24.3 0.1 pad_add_fusion
  24.4 0.2 select_reduce_fusion
  24.6 0.1 copy.16
  24.8 0.8 copy.19.ids_ref
  25.5 0.6 fusion.9.scale_ref
  26.2 9.4 %modal_local.1 = (f32[192,2048]{1,0:T(8,128)}, f32[192,2048]{1,0:T(8,128)}, bf16[2,16,8,128]{3,2,1,0:T(8,128)(2,1)}) custom-call(s32[208,1]{1,0:T(8,128)} %copy.19.ids_ref, f32[208,1]{1,0:T(8,128)} %fusion.9.scale_ref, bf16[512,2048]{1,0:T(8,128)(2,1)} %table_ref.1, f32[1,2048]{1,0:T(1,128)} %bitcast.36, f32[9,2048]{1,0:T(8,128)} %reshape.80.taps_ref, ...), custom_call_target="tpu_custom_call" | custom-call | tf_op jit(solution)/shard_map/modal_local/pallas_call | solution.py:475
  35.6 16.0 %shard_map.114 = bf16[8,256,128]{2,1,0:T(8,128)(2,1)} custom-call(bf16[256,128]{1,0:T(8,128)(2,1)} %bitcast.34), custom_call_target="tpu_custom_call" | custom-call | tf_op jit(solution)/shard_map/pallas_call | solution.py:354
  51.6 4.8 %modal_finish.1 = (bf16[192,2048]{1,0:T(8,128)(2,1)}, bf16[192,2048]{1,0:T(8,128)(2,1)}, f32[192,128]{1,0:T(8,128)}) custom-call(s32[1]{0:T(128)} %bitcast.rank_ref, bf16[8,2,16,8,128]{4,3,2,1,0:T(8,128)(2,1)} %bitcast.29, f32[2,16,8,128]{3,2,1,0:T(8,128)} %get-tuple-element.23.decay_ref, f32[2,16,8,128]{3,2,1,0:T(8,128)} %get-tuple-element.22.residue_ref, ...), custom_call_target="tpu_custom_call" | custom-call | tf_op jit(solution)/shard_map/modal_finish/pallas_call | solution.py:479
  56.4 1.0 reduce_sum.48
  57.4 0.6 pad_bitcast_fusion.small_ref
  58.0 32.4 %shard_map.115 = (bf16[192,8192]{1,0:T(8,128)(2,1)}, f32[4,8,128]{2,1,0:T(8,128)}) custom-call(bf16[192,2048]{1,0:T(8,128)(2,1)} %get-tuple-element.14.in_ref, f32[8,128]{1,0:T(8,128)} %pad_bitcast_fusion.small_ref), custom_call_target="tpu_custom_call" | custom-call | tf_op jit(solution)/shard_map/pallas_call | solution.py:334
  90.4 0.7 reduce_sum.49
  91.1 0.0 all-gather.2.cloned.1.call-done
  91.2 5.5 %convolution_multiply_fusion = f32[192,384]{1,0:T(8,128)S(1)} fusion(bf16[192,8192]{1,0:T(8,128)(2,1)} %get-tuple-element.16, bf16[8192,384]{1,0:T(8,128)(2,1)} %all-gather.2.cloned.1.call-done, f32[192]{0:T(256)S(1)} %add_rsqrt_fusion), kind=kOutput, calls=%fused_computation.1 | convolution fusion | flops 1208033280 | bytes 9732864 | tf_op jit(solution)/shard_map/dot_general | solution.py:510
  96.7 0.5 fusion.17
  97.2 0.8 concatenate.8.in_ref
  98.0 22.1 %shard_map.116 = bf16[8,192,384]{2,1,0:T(8,128)(2,1)} custom-call(bf16[192,384]{1,0:T(8,128)(2,1)} %concatenate.8.in_ref), custom_call_target="tpu_custom_call" | custom-call | tf_op jit(solution)/shard_map/pallas_call | solution.py:354
  120.1 3.0 %attend.1 = bf16[192,128]{1,0:T(8,128)(2,1)} custom-call(s32[2]{0:T(128)} %dynamic_slice.3.blocks_ref, bf16[1536,384]{1,0:T(8,128)(2,1)} %bitcast.28), custom_call_target="tpu_custom_call" | custom-call | tf_op jit(solution)/shard_map/attend/pallas_call | solution.py:528
  (14 shorter events, 0.1 us)
Async XLA Ops:
  7.2 17.2 %copy-start.2 = (s32[192]{0:T(256)S(1)}, s32[192]{0:T(256)}, u32[]{:S(2)}) copy-start(s32[192]{0:T(256)} %param.10) | copy-start | bytes 2308
  7.2 14.3 %copy-start = (f32[16,2048]{1,0:T(8,128)S(1)}, f32[16,2048]{1,0:T(8,128)}, u32[]{:S(2)}) copy-start(f32[16,2048]{1,0:T(8,128)} %param.16) | copy-start | bytes 393220
  7.2 14.4 %copy-start.1 = (f32[3,3,2048]{2,1,0:T(4,128)S(1)}, f32[3,3,2048]{2,1,0:T(4,128)}, u32[]{:S(2)}) copy-start(f32[3,3,2048]{2,1,0:T(4,128)} %param.14) | copy-start | bytes 221188
  7.2 16.6 %copy-start.3 = (s32[16]{0:T(128)S(1)}, s32[16]{0:T(128)}, u32[]{:S(2)}) copy-start(s32[16]{0:T(128)} %param.11) | copy-start | bytes 196
  7.2 83.9 %all-gather.2.cloned.1.call-start = ((), (), s32[]{:S(2)}) async-start(), calls=%async_computation | async-start | bytes 7077888 | tf_op jit(solution)/shard_map/all_gather | solution.py:423
  8.7 15.6 %collective-permute-start = (s32[16]{0:T(128)S(1)}, s32[16]{0:T(128)S(1)}, u32[]{:S(2)}, u32[]{:S(2)}) collective-permute-start(s32[16]{0:T(128)S(1)} %slice.32), channel_id=1, source_target_pairs={{0,4},{4,8},{8,12},{12,16},{16,20},{20,24},{24,28},{1,5},{5,9},{9,... | collective-permute-start | bytes 200 | tf_op jit(solution)/shard_map/ppermute | solution.py:424
Sparse Core Ops, SparseCore 0:
  9.7 72.8 all-gather.1

commit v4 on v3

--- a/solution.py
+++ b/solution.py
@@ -254,54 +254,110 @@
         copy.wait()
 
 
-def paired_kernel(axis, in_ref, out_ref, send, recv, hand_send, hand_recv, own):
+def paired_kernel(axis, pieces, in_ref, out_ref, send, recv, hand_send, hand_recv, own):
     size, me = lax.axis_size(axis), lax.axis_index(axis)
     chips = size // 2
     chip, core = lax.div(me, 2), lax.rem(me, 2)
     sibling = me + 1 - 2 * core
-    peers = [sibling] + [lax.rem(chip + d, chips) * 2 + core for d in range(1, chips)]
+    ways = ((1, chip < chips - 1), (-1, chip > 0))
     barrier = pltpu.get_barrier_semaphore()
-    for peer in peers:
+
+    def greet(peer):
         pl.semaphore_signal(
             barrier, inc=1, device_id={axis: peer}, device_id_type=pl.DeviceIdType.MESH
         )
-    pl.semaphore_wait(barrier, chips)
-    copies = [
-        pltpu.make_async_remote_copy(
-            src_ref=in_ref,
-            dst_ref=out_ref.at[me],
-            send_sem=send.at[d],
-            recv_sem=recv.at[d],
-            device_id={axis: peers[d]},
+
+    greet(sibling)
+    for way, open_ in ways:
+        pl.when(open_)(functools.partial(greet, me + 2 * way))
+    for count in (2, 3):
+        inner = (chip > 0) & (chip < chips - 1)
+        pl.when(inner if count == 3 else jnp.logical_not(inner))(
+            functools.partial(pl.semaphore_wait, barrier, count)
+        )
+    rows = in_ref.shape[0] // pieces
+
+    def remote(source, owner, part, sends, recvs, spot, peer):
+        return pltpu.make_async_remote_copy(
+            src_ref=source,
+            dst_ref=out_ref.at[owner, part * rows : (part + 1) * rows],
+            send_sem=sends.at[spot],
+            recv_sem=recvs.at[spot],
+            device_id={axis: peer},
             device_id_type=pl.DeviceIdType.MESH,
         )
-        for d in range(chips)
-    ]
-    for copy in copies[1:]:
-        copy.start()
-    copies[0].start()
+
+    def block(owner, part):
+        return out_ref.at[owner, part * rows : (part + 1) * rows]
+
+    def outgoing(w, d, part):
+        way = ways[w][0]
+        owner = me - 2 * way * (d - 1)
+        source = in_ref.at[part * rows : (part + 1) * rows] if d == 1 else block(owner, part)
+        return remote(source, owner, part, send, recv, (w, d - 1, part), me + 2 * way)
+
+    def incoming(w, d, part):
+        owner = me - 2 * ways[w][0] * d
+        return remote(
+            block(owner, part), owner, part, send, recv, (w, d - 1, part), sibling
+        )
+
+    def handed(w, d, part):
+        owner = me - 2 * ways[w][0] * d
+        return remote(
+            block(owner, part), owner, part, hand_send, hand_recv, (w, d, part), sibling
+        )
+
+    def arrives(w, d):
+        return chip >= d if w == 0 else chip + d < chips
+
+    for part in range(pieces):
+        for w in range(2):
+            pl.when(ways[w][1])(lambda w=w, part=part: outgoing(w, 1, part).start())
+    for part in range(pieces):
+        remote(
+            in_ref.at[part * rows : (part + 1) * rows],
+            me,
+            part,
+            hand_send,
+            hand_recv,
+            (0, 0, part),
+            sibling,
+        ).start()
     mine = pltpu.make_async_copy(in_ref, out_ref.at[me], own)
     mine.start()
-    hands = []
+
+    def relay(w, d, part):
+        incoming(w, d, part).wait_recv()
+        if d < chips - 1:
+            pl.when(ways[w][1])(lambda: outgoing(w, d + 1, part).start())
+        handed(w, d, part).start()
+
     for d in range(1, chips):
-        copies[d].wait_recv()
-        source = lax.rem(chip + chips - d, chips) * 2 + core
-        hand = pltpu.make_async_remote_copy(
-            src_ref=out_ref.at[source],
-            dst_ref=out_ref.at[source],
-            send_sem=hand_send.at[d],
-            recv_sem=hand_recv.at[d],
-            device_id={axis: sibling},
-            device_id_type=pl.DeviceIdType.MESH,
-        )
-        hand.start()
-        hands.append(hand)
+        for part in range(pieces):
+            for w in range(2):
+                pl.when(arrives(w, d))(functools.partial(relay, w, d, part))
     mine.wait()
-    copies[0].wait_recv()
-    for copy in copies:
-        copy.wait_send()
-    for hand in hands:
-        hand.wait()
+    for part in range(pieces):
+        remote(
+            in_ref.at[part * rows : (part + 1) * rows],
+            me,
+            part,
+            hand_send,
+            hand_recv,
+            (0, 0, part),
+            sibling,
+        ).wait()
+        for w in range(2):
+            pl.when(ways[w][1])(lambda w=w, part=part: outgoing(w, 1, part).wait_send())
+            for d in range(1, chips):
+
+                def finish(w=w, d=d, part=part):
+                    handed(w, d, part).wait()
+                    if d < chips - 1:
+                        pl.when(ways[w][1])(lambda: outgoing(w, d + 1, part).wait_send())
+
+                pl.when(arrives(w, d))(finish)
 
 
 def gather_direct(axis, arrays, columns, collective_id):
@@ -350,13 +406,13 @@
     size = lax.axis_size(axis)
     vmem = pl.BlockSpec(memory_space=pltpu.VMEM)
     dma = pltpu.SemaphoreType.DMA
-    chips = size // 2
+    chips, pieces = size // 2, 2
     return pl.pallas_call(
-        functools.partial(paired_kernel, axis),
+        functools.partial(paired_kernel, axis, pieces),
         in_specs=[vmem],
         out_specs=vmem,
         out_shape=jax.ShapeDtypeStruct((size,) + array.shape, array.dtype),
-        scratch_shapes=[dma((chips,)), dma((chips,)), dma((chips,)), dma((chips,)), dma(())],
+        scratch_shapes=[dma((2, chips, pieces))] * 4 + [dma(())],
         compiler_params=pltpu.CompilerParams(
             collective_id=collective_id, has_side_effects=True
         ),

time: 131 us -> 132 us (level)
  Pallas kernels: 94.5 us -> 95.9 us
    pallas_call x2, Pallas kernels: 38.1 us -> 39.6 us  [gather_paired(): pl.pallas_call(functools.partial(paired_kernel, axis, pieces), in_specs=[...]
  transfers between devices with their start and end apart: 2 -> 2, of which waited for: 0 -> 0; matrix products, arithmetic and copies ran while one was open for 9% -> 9% of each run, Pallas kernels for 53% -> 59%
where the time goes in v4:
time: 132 us; the launch traced here: 131 us
  Pallas kernels  95.9 us (73%)
  between operations  14.2 us (11%)
  local copies, waits for them, and re-layouts  6.64 us (5%)
  other arithmetic  5.97 us (5%)
  matrix products  5.54 us (4%)
  starting transfers between devices  2.42 us (2%)
    pallas_call x2, Pallas kernels, gather_paired(): pl.pallas_call(functools.partial(paired_kernel, axis, pieces), in_specs=[...  39.6 us
    pallas_call x1, Pallas kernels, gather_square(): pl.pallas_call(functools.partial(square_kernel, axis), in_specs=[vmem, vm...  32.3 us
    pallas_call x1, Pallas kernels, shards(): query, base, state = local(*local_args)  9.42 us
    pallas_call x1, Pallas kernels, gather_direct(): pl.pallas_call(functools.partial(direct_kernel, axis, columns, count), in...  6.8 us
    dot_general x1, matrix products, shards(): jnp.dot(scaled_full, weights_full, preferred_element_type=jnp.float32)  5.54 us
    pallas_call x1, Pallas kernels, shards(): pl.pallas_call(modal_finish, grid_spec=pltpu.PrefetchScalarGridSpec(num_s...  4.84 us
    pallas_call x1, Pallas kernels, shards(): pl.pallas_call(attend, in_specs=[pl.BlockSpec(memory_space=pltpu.SMEM), p...  3.02 us
  transfers between devices with their start and end apart: 2, of which 0 were waited for; matrix products, arithmetic and copies ran while one was open for 9% of the time, Pallas kernels for 59%

profile of v4, /device:TPU:0, one launch (start us, length us, event | category | flops | bytes accessed | tf_op | source)
XLA Modules:
  0.0 131.4 jit_solution(8996878252122885329)
XLA Ops:
  7.2 0.0 all-gather.2.cloned.1.call-start
  7.2 0.7 all-gather.2.cloned.1.call-update
  7.9 0.8 slice.32
  8.7 2.4 %collective-permute-start = (s32[16]{0:T(128)S(1)}, s32[16]{0:T(128)S(1)}, u32[]{:S(2)}, u32[]{:S(2)}) collective-permute-start(s32[16]{0:T(128)S(1)} %slice.32), channel_id=1, source_target_pairs={{0,4},{4,8},{8,12},{12,16},{16,20},{20,24},{24,28},{1,5},{5,9},{9,... | collective-permute-start | bytes 200 | tf_op jit(solution)/shard_map/ppermute | solution.py:480
  11.1 2.1 %multiply_reduce_fusion = f32[512]{0:T(512)S(1)} fusion(bf16[512,2048]{1,0:T(8,128)(2,1)} %table_ref.1), kind=kLoop, calls=%fused_computation | loop fusion | flops 3145216 | bytes 2099200 | tf_op jit(solution)/shard_map/reduce_sum | solution.py:486
  13.2 0.6 pad_bitcast_fusion.1.refs_0_
  13.8 6.8 %shard_map.113 = f32[4,8,128]{2,1,0:T(8,128)} custom-call(f32[8,128]{1,0:T(8,128)} %pad_bitcast_fusion.1.refs_0_), custom_call_target="tpu_custom_call" | custom-call | tf_op jit(solution)/shard_map/pallas_call | solution.py:367
  20.6 0.9 copy.20
  21.5 0.0 copy-done
  21.6 0.7 reshape.80.taps_ref
  22.3 0.7 reduce_sum.46
  23.0 0.7 copy_bitcast_fusion
  23.8 0.6 dynamic_slice.3.blocks_ref
  24.3 0.0 collective-permute-done
  24.3 0.1 pad_add_fusion
  24.4 0.2 select_reduce_fusion
  24.6 0.1 copy.16
  24.8 0.8 copy.19.ids_ref
  25.5 0.6 fusion.9.scale_ref
  26.2 9.4 %modal_local.1 = (f32[192,2048]{1,0:T(8,128)}, f32[192,2048]{1,0:T(8,128)}, bf16[2,16,8,128]{3,2,1,0:T(8,128)(2,1)}) custom-call(s32[208,1]{1,0:T(8,128)} %copy.19.ids_ref, f32[208,1]{1,0:T(8,128)} %fusion.9.scale_ref, bf16[512,2048]{1,0:T(8,128)(2,1)} %table_ref.1, f32[1,2048]{1,0:T(1,128)} %bitcast.36, f32[9,2048]{1,0:T(8,128)} %reshape.80.taps_ref, ...), custom_call_target="tpu_custom_call" | custom-call | tf_op jit(solution)/shard_map/modal_local/pallas_call | solution.py:531
  35.6 23.8 %shard_map.114 = bf16[8,256,128]{2,1,0:T(8,128)(2,1)} custom-call(bf16[256,128]{1,0:T(8,128)(2,1)} %bitcast.34), custom_call_target="tpu_custom_call" | custom-call | tf_op jit(solution)/shard_map/pallas_call | solution.py:410
  59.4 4.8 %modal_finish.1 = (bf16[192,2048]{1,0:T(8,128)(2,1)}, bf16[192,2048]{1,0:T(8,128)(2,1)}, f32[192,128]{1,0:T(8,128)}) custom-call(s32[1]{0:T(128)} %bitcast.rank_ref, bf16[8,2,16,8,128]{4,3,2,1,0:T(8,128)(2,1)} %bitcast.29, f32[2,16,8,128]{3,2,1,0:T(8,128)} %get-tuple-element.23.decay_ref, f32[2,16,8,128]{3,2,1,0:T(8,128)} %get-tuple-element.22.residue_ref, ...), custom_call_target="tpu_custom_call" | custom-call | tf_op jit(solution)/shard_map/modal_finish/pallas_call | solution.py:535
  64.2 1.0 reduce_sum.48
  65.2 0.6 pad_bitcast_fusion.small_ref
  65.8 32.3 %shard_map.115 = (bf16[192,8192]{1,0:T(8,128)(2,1)}, f32[4,8,128]{2,1,0:T(8,128)}) custom-call(bf16[192,2048]{1,0:T(8,128)(2,1)} %get-tuple-element.14.in_ref, f32[8,128]{1,0:T(8,128)} %pad_bitcast_fusion.small_ref), custom_call_target="tpu_custom_call" | custom-call | tf_op jit(solution)/shard_map/pallas_call | solution.py:390
  98.1 0.7 reduce_sum.49
  98.8 0.0 all-gather.2.cloned.1.call-done
  98.8 5.5 %convolution_multiply_fusion = f32[192,384]{1,0:T(8,128)S(1)} fusion(bf16[192,8192]{1,0:T(8,128)(2,1)} %get-tuple-element.16, bf16[8192,384]{1,0:T(8,128)(2,1)} %all-gather.2.cloned.1.call-done, f32[192]{0:T(256)S(1)} %add_rsqrt_fusion), kind=kOutput, calls=%fused_computation.1 | convolution fusion | flops 1208033280 | bytes 9732864 | tf_op jit(solution)/shard_map/dot_general | solution.py:566
  104.4 0.5 fusion.17
  104.9 0.8 concatenate.8.in_ref
  105.7 15.8 %shard_map.116 = bf16[8,192,384]{2,1,0:T(8,128)(2,1)} custom-call(bf16[192,384]{1,0:T(8,128)(2,1)} %concatenate.8.in_ref), custom_call_target="tpu_custom_call" | custom-call | tf_op jit(solution)/shard_map/pallas_call | solution.py:410
  121.5 3.0 %attend.1 = bf16[192,128]{1,0:T(8,128)(2,1)} custom-call(s32[2]{0:T(128)} %dynamic_slice.3.blocks_ref, bf16[1536,384]{1,0:T(8,128)(2,1)} %bitcast.28), custom_call_target="tpu_custom_call" | custom-call | tf_op jit(solution)/shard_map/attend/pallas_call | solution.py:584
  (14 shorter events, 0.1 us)
Async XLA Ops:
  7.2 17.2 %copy-start.2 = (s32[192]{0:T(256)S(1)}, s32[192]{0:T(256)}, u32[]{:S(2)}) copy-start(s32[192]{0:T(256)} %param.10) | copy-start | bytes 2308
  7.2 14.3 %copy-start = (f32[16,2048]{1,0:T(8,128)S(1)}, f32[16,2048]{1,0:T(8,128)}, u32[]{:S(2)}) copy-start(f32[16,2048]{1,0:T(8,128)} %param.16) | copy-start | bytes 393220
  7.2 14.4 %copy-start.1 = (f32[3,3,2048]{2,1,0:T(4,128)S(1)}, f32[3,3,2048]{2,1,0:T(4,128)}, u32[]{:S(2)}) copy-start(f32[3,3,2048]{2,1,0:T(4,128)} %param.14) | copy-start | bytes 221188
  7.2 16.6 %copy-start.3 = (s32[16]{0:T(128)S(1)}, s32[16]{0:T(128)}, u32[]{:S(2)}) copy-start(s32[16]{0:T(128)} %param.11) | copy-start | bytes 196
  7.2 91.6 %all-gather.2.cloned.1.call-start = ((), (), s32[]{:S(2)}) async-start(), calls=%async_computation | async-start | bytes 7077888 | tf_op jit(solution)/shard_map/all_gather | solution.py:479
  8.7 15.6 %collective-permute-start = (s32[16]{0:T(128)S(1)}, s32[16]{0:T(128)S(1)}, u32[]{:S(2)}, u32[]{:S(2)}) collective-permute-start(s32[16]{0:T(128)S(1)} %slice.32), channel_id=1, source_target_pairs={{0,4},{4,8},{8,12},{12,16},{16,20},{20,24},{24,28},{1,5},{5,9},{9,... | collective-permute-start | bytes 200 | tf_op jit(solution)/shard_map/ppermute | solution.py:480
Sparse Core Ops, SparseCore 0:
  9.7 70.0 all-gather.1

commit v5 on v4

--- a/solution.py
+++ b/solution.py
@@ -360,6 +360,56 @@
                 pl.when(arrives(w, d))(finish)
 
 
+def star_kernel(axis, in_ref, out_ref, send, recv, hand_send, hand_recv, own):
+    size, me = lax.axis_size(axis), lax.axis_index(axis)
+    chips = size // 2
+    chip, core = lax.div(me, 2), lax.rem(me, 2)
+    sibling = me + 1 - 2 * core
+    peers = [sibling] + [lax.rem(chip + d, chips) * 2 + core for d in range(1, chips)]
+    barrier = pltpu.get_barrier_semaphore()
+    for peer in peers:
+        pl.semaphore_signal(
+            barrier, inc=1, device_id={axis: peer}, device_id_type=pl.DeviceIdType.MESH
+        )
+    pl.semaphore_wait(barrier, chips)
+    copies = [
+        pltpu.make_async_remote_copy(
+            src_ref=in_ref,
+            dst_ref=out_ref.at[me],
+            send_sem=send.at[d],
+            recv_sem=recv.at[d],
+            device_id={axis: peers[d]},
+            device_id_type=pl.DeviceIdType.MESH,
+        )
+        for d in range(chips)
+    ]
+    for copy in copies[1:]:
+        copy.start()
+    copies[0].start()
+    mine = pltpu.make_async_copy(in_ref, out_ref.at[me], own)
+    mine.start()
+    hands = []
+    for d in range(1, chips):
+        copies[d].wait_recv()
+        source = lax.rem(chip + chips - d, chips) * 2 + core
+        hand = pltpu.make_async_remote_copy(
+            src_ref=out_ref.at[source],
+            dst_ref=out_ref.at[source],
+            send_sem=hand_send.at[d],
+            recv_sem=hand_recv.at[d],
+            device_id={axis: sibling},
+            device_id_type=pl.DeviceIdType.MESH,
+        )
+        hand.start()
+        hands.append(hand)
+    mine.wait()
+    copies[0].wait_recv()
+    for copy in copies:
+        copy.wait_send()
+    for hand in hands:
+        hand.wait()
+
+
 def gather_direct(axis, arrays, columns, collective_id):
     size, count = lax.axis_size(axis), len(arrays)
     vmem = pl.BlockSpec(memory_space=pltpu.VMEM)
@@ -413,6 +463,23 @@
         out_specs=vmem,
         out_shape=jax.ShapeDtypeStruct((size,) + array.shape, array.dtype),
         scratch_shapes=[dma((2, chips, pieces))] * 4 + [dma(())],
+        compiler_params=pltpu.CompilerParams(
+            collective_id=collective_id, has_side_effects=True
+        ),
+    )(array)
+
+
+def gather_star(axis, array, collective_id):
+    size = lax.axis_size(axis)
+    vmem = pl.BlockSpec(memory_space=pltpu.VMEM)
+    dma = pltpu.SemaphoreType.DMA
+    chips = size // 2
+    return pl.pallas_call(
+        functools.partial(star_kernel, axis),
+        in_specs=[vmem],
+        out_specs=vmem,
+        out_shape=jax.ShapeDtypeStruct((size,) + array.shape, array.dtype),
+        scratch_shapes=[dma((chips,)), dma((chips,)), dma((chips,)), dma((chips,)), dma(())],
         compiler_params=pltpu.CompilerParams(
             collective_id=collective_id, has_side_effects=True
         ),
@@ -529,7 +596,7 @@
         skip_gain[None],
     )
     query, base, state = local(*local_args)
-    states = gather_paired(
+    states = gather_star(
         "ctx", state.reshape(spans * ORDER * tiles, 128), 2
     ).reshape(nctx, spans, ORDER, tiles, 128)
     mixed, scaled, lanes = pl.pallas_call(

time: 132 us -> 130 us (0.985)
  Pallas kernels: 95.9 us -> 94.3 us
    pallas_call x2 -> x1, Pallas kernels: 39.6 us -> 21.9 us  [gather_paired(): pl.pallas_call(functools.partial(paired_kernel, axis, pieces), in_specs=[...]
    pallas_call x0 -> x1, Pallas kernels: none -> 16 us  [gather_star(): pl.pallas_call(functools.partial(star_kernel, axis), in_specs=[vmem], out...]
  transfers between devices with their start and end apart: 2 -> 2, of which waited for: 0 -> 0; matrix products, arithmetic and copies ran while one was open for 9% -> 9% of each run, Pallas kernels for 59% -> 53%
where the time goes in v5:
time: 130 us
  Pallas kernels  94.3 us (73%)
  between operations  14.2 us (11%)
  local copies, waits for them, and re-layouts  6.64 us (5%)
  other arithmetic  5.96 us (5%)
  matrix products  5.54 us (4%)
  starting transfers between devices  2.42 us (2%)
    pallas_call x1, Pallas kernels, gather_square(): pl.pallas_call(functools.partial(square_kernel, axis), in_specs=[vmem, vm...  32.4 us
    pallas_call x1, Pallas kernels, gather_paired(): pl.pallas_call(functools.partial(paired_kernel, axis, pieces), in_specs=[...  21.9 us
    pallas_call x1, Pallas kernels, gather_star(): pl.pallas_call(functools.partial(star_kernel, axis), in_specs=[vmem], out...  16 us
    pallas_call x1, Pallas kernels, shards(): query, base, state = local(*local_args)  9.42 us
    pallas_call x1, Pallas kernels, gather_direct(): pl.pallas_call(functools.partial(direct_kernel, axis, columns, count), in...  6.8 us
    dot_general x1, matrix products, shards(): jnp.dot(scaled_full, weights_full, preferred_element_type=jnp.float32)  5.54 us
    pallas_call x1, Pallas kernels, shards(): pl.pallas_call(modal_finish, grid_spec=pltpu.PrefetchScalarGridSpec(num_s...  4.8 us
    pallas_call x1, Pallas kernels, shards(): pl.pallas_call(attend, in_specs=[pl.BlockSpec(memory_space=pltpu.SMEM), p...  3.02 us
  transfers between devices with their start and end apart: 2, of which 0 were waited for; matrix products, arithmetic and copies ran while one was open for 9% of the time, Pallas kernels for 53%

profile of v5, /device:TPU:0, one launch (start us, length us, event | category | flops | bytes accessed | tf_op | source)
XLA Modules:
  0.0 129.8 jit_solution(4082326401596360033)
XLA Ops:
  7.2 0.0 all-gather.2.cloned.1.call-start
  7.2 0.7 all-gather.2.cloned.1.call-update
  7.9 0.8 slice.32
  8.7 2.4 %collective-permute-start = (s32[16]{0:T(128)S(1)}, s32[16]{0:T(128)S(1)}, u32[]{:S(2)}, u32[]{:S(2)}) collective-permute-start(s32[16]{0:T(128)S(1)} %slice.32), channel_id=1, source_target_pairs={{0,4},{4,8},{8,12},{12,16},{16,20},{20,24},{24,28},{1,5},{5,9},{9,... | collective-permute-start | bytes 200 | tf_op jit(solution)/shard_map/ppermute | solution.py:547
  11.1 2.1 %multiply_reduce_fusion = f32[512]{0:T(512)S(1)} fusion(bf16[512,2048]{1,0:T(8,128)(2,1)} %table_ref.1), kind=kLoop, calls=%fused_computation | loop fusion | flops 3145216 | bytes 2099200 | tf_op jit(solution)/shard_map/reduce_sum | solution.py:553
  13.2 0.6 pad_bitcast_fusion.1.refs_0_
  13.8 6.8 %shard_map.113 = f32[4,8,128]{2,1,0:T(8,128)} custom-call(f32[8,128]{1,0:T(8,128)} %pad_bitcast_fusion.1.refs_0_), custom_call_target="tpu_custom_call" | custom-call | tf_op jit(solution)/shard_map/pallas_call | solution.py:417
  20.6 0.9 copy.20
  21.5 0.0 copy-done
  21.6 0.7 reshape.80.taps_ref
  22.3 0.7 reduce_sum.46
  23.0 0.7 copy_bitcast_fusion
  23.8 0.6 dynamic_slice.3.blocks_ref
  24.3 0.0 collective-permute-done
  24.3 0.1 pad_add_fusion
  24.4 0.2 select_reduce_fusion
  24.6 0.1 copy.16
  24.8 0.8 copy.19.ids_ref
  25.5 0.6 fusion.9.scale_ref
  26.2 9.4 %modal_local.1 = (f32[192,2048]{1,0:T(8,128)}, f32[192,2048]{1,0:T(8,128)}, bf16[2,16,8,128]{3,2,1,0:T(8,128)(2,1)}) custom-call(s32[208,1]{1,0:T(8,128)} %copy.19.ids_ref, f32[208,1]{1,0:T(8,128)} %fusion.9.scale_ref, bf16[512,2048]{1,0:T(8,128)(2,1)} %table_ref.1, f32[1,2048]{1,0:T(1,128)} %bitcast.36, f32[9,2048]{1,0:T(8,128)} %reshape.80.taps_ref, ...), custom_call_target="tpu_custom_call" | custom-call | tf_op jit(solution)/shard_map/modal_local/pallas_call | solution.py:598
  35.6 16.0 %shard_map.114 = bf16[8,256,128]{2,1,0:T(8,128)(2,1)} custom-call(bf16[256,128]{1,0:T(8,128)(2,1)} %bitcast.34), custom_call_target="tpu_custom_call" | custom-call | tf_op jit(solution)/shard_map/pallas_call | solution.py:477
  51.6 4.8 %modal_finish.1 = (bf16[192,2048]{1,0:T(8,128)(2,1)}, bf16[192,2048]{1,0:T(8,128)(2,1)}, f32[192,128]{1,0:T(8,128)}) custom-call(s32[1]{0:T(128)} %bitcast.rank_ref, bf16[8,2,16,8,128]{4,3,2,1,0:T(8,128)(2,1)} %bitcast.29, f32[2,16,8,128]{3,2,1,0:T(8,128)} %get-tuple-element.23.decay_ref, f32[2,16,8,128]{3,2,1,0:T(8,128)} %get-tuple-element.22.residue_ref, ...), custom_call_target="tpu_custom_call" | custom-call | tf_op jit(solution)/shard_map/modal_finish/pallas_call | solution.py:602
  56.4 1.0 reduce_sum.48
  57.4 0.6 pad_bitcast_fusion.small_ref
  58.0 32.4 %shard_map.115 = (bf16[192,8192]{1,0:T(8,128)(2,1)}, f32[4,8,128]{2,1,0:T(8,128)}) custom-call(bf16[192,2048]{1,0:T(8,128)(2,1)} %get-tuple-element.14.in_ref, f32[8,128]{1,0:T(8,128)} %pad_bitcast_fusion.small_ref), custom_call_target="tpu_custom_call" | custom-call | tf_op jit(solution)/shard_map/pallas_call | solution.py:440
  90.4 0.7 reduce_sum.49
  91.1 0.0 all-gather.2.cloned.1.call-done
  91.2 5.5 %convolution_multiply_fusion = f32[192,384]{1,0:T(8,128)S(1)} fusion(bf16[192,8192]{1,0:T(8,128)(2,1)} %get-tuple-element.16, bf16[8192,384]{1,0:T(8,128)(2,1)} %all-gather.2.cloned.1.call-done, f32[192]{0:T(256)S(1)} %add_rsqrt_fusion), kind=kOutput, calls=%fused_computation.1 | convolution fusion | flops 1208033280 | bytes 9732864 | tf_op jit(solution)/shard_map/dot_general | solution.py:633
  96.7 0.5 fusion.17
  97.2 0.8 concatenate.8.in_ref
  98.0 21.9 %shard_map.116 = bf16[8,192,384]{2,1,0:T(8,128)(2,1)} custom-call(bf16[192,384]{1,0:T(8,128)(2,1)} %concatenate.8.in_ref), custom_call_target="tpu_custom_call" | custom-call | tf_op jit(solution)/shard_map/pallas_call | solution.py:460
  119.9 3.0 %attend.1 = bf16[192,128]{1,0:T(8,128)(2,1)} custom-call(s32[2]{0:T(128)} %dynamic_slice.3.blocks_ref, bf16[1536,384]{1,0:T(8,128)(2,1)} %bitcast.28), custom_call_target="tpu_custom_call" | custom-call | tf_op jit(solution)/shard_map/attend/pallas_call | solution.py:651
  (14 shorter events, 0.1 us)
Async XLA Ops:
  7.2 17.2 %copy-start.2 = (s32[192]{0:T(256)S(1)}, s32[192]{0:T(256)}, u32[]{:S(2)}) copy-start(s32[192]{0:T(256)} %param.10) | copy-start | bytes 2308
  7.2 14.3 %copy-start = (f32[16,2048]{1,0:T(8,128)S(1)}, f32[16,2048]{1,0:T(8,128)}, u32[]{:S(2)}) copy-start(f32[16,2048]{1,0:T(8,128)} %param.16) | copy-start | bytes 393220
  7.2 14.4 %copy-start.1 = (f32[3,3,2048]{2,1,0:T(4,128)S(1)}, f32[3,3,2048]{2,1,0:T(4,128)}, u32[]{:S(2)}) copy-start(f32[3,3,2048]{2,1,0:T(4,128)} %param.14) | copy-start | bytes 221188
  7.2 16.6 %copy-start.3 = (s32[16]{0:T(128)S(1)}, s32[16]{0:T(128)}, u32[]{:S(2)}) copy-start(s32[16]{0:T(128)} %param.11) | copy-start | bytes 196
  7.2 83.9 %all-gather.2.cloned.1.call-start = ((), (), s32[]{:S(2)}) async-start(), calls=%async_computation | async-start | bytes 7077888 | tf_op jit(solution)/shard_map/all_gather | solution.py:546
  8.7 15.6 %collective-permute-start = (s32[16]{0:T(128)S(1)}, s32[16]{0:T(128)S(1)}, u32[]{:S(2)}, u32[]{:S(2)}) collective-permute-start(s32[16]{0:T(128)S(1)} %slice.32), channel_id=1, source_target_pairs={{0,4},{4,8},{8,12},{12,16},{16,20},{20,24},{24,28},{1,5},{5,9},{9,... | collective-permute-start | bytes 200 | tf_op jit(solution)/shard_map/ppermute | solution.py:547
Sparse Core Ops, SparseCore 0:
  9.7 72.8 all-gather.1
